TPU v7x, 256 devices: a whole 4x4x8 slice. The times are simulated.
256 devices in a mesh: dp: 2 (over z_lo), tensor: 128 (over x, y, z_hi, core).
Axes of the slice: x: 4, y: 4, z: 8 (z_hi: 4, z_lo: 2; z = z_hi * 2 + z_lo), core: 2. Of those that a mesh axis runs over, the one named last changes fastest.
Arguments:
- tokens: bfloat16 [2, 16384, 4096], P('dp', 'tensor'), may hold values from -35 to 35
- norm_gain: float32 [4096], replicated, may hold values from 0.1 to 1.9
- segments: int32 [2, 16384], P('dp', 'tensor'), may hold values from 0 to 7, never falling along the last dimension, each value on 1 to 8192 neighbouring positions
- deal_table: int32 [128, 2], P('tensor'), may hold values from 0 to 1, each once within a row
- projection: bfloat16 [32768, 768], P('tensor'), may hold values from -1 to 1
Outputs:
- context: bfloat16 [2, 16384, 4096], P('dp', 'tensor')
- key_cache: bfloat16 [2, 8, 16384, 128], P('dp', None, 'tensor')
- value_cache: bfloat16 [2, 8, 16384, 128], P('dp', None, 'tensor')
Inputs may be any that keep to these rules, and one draw needn't show every extreme that they name: `segments`: segment ids never fall along a buffer; every id appears, each on at most 8192 positions, one on exactly 8192. `deal_table`: each row names every group once.
All inputs are finite; a program needn't handle non-finite values.
Results may differ from a plain program's by a relative error of at most 0.0082.
Values may be sent and summed in bfloat16 or wider, within the bound.
A program may use at most 128 MiB of HBM per device.

v0:
```python
import jax
import jax.numpy as jnp
from jax import lax
from jax.sharding import PartitionSpec as P

QUERY_HEADS = 32
KEY_VALUE_HEADS = 8
HEAD_SIZE = 128
NSEG = 8
WINDOW = 512
SINKS = 4


rope_base = 500000.0
norm_eps = 1e-05


def from_partner(value, axis, apart):
    mask = 2**apart
    pairs = [(source, source ^ mask) for source in range(lax.axis_size(axis))]
    return lax.ppermute(value, axis, pairs)


def shifted(block, axis, distance):
    devices = range(lax.axis_size(axis))
    route = [(i - distance, i) for i in devices if i - distance in devices]
    return lax.ppermute(block, axis, route)


def stack_pair(holding, arrived, upper_flag, axis_pos):
    lower_part = jnp.where(upper_flag, arrived, holding)
    upper_part = jnp.where(upper_flag, holding, arrived)
    return jnp.stack((lower_part, upper_part), axis=axis_pos)


def rotary(values, angles):
    half_width = values.shape[-1] // 2
    first_half = values[..., :half_width]
    second_half = values[..., half_width:]
    cosine = jnp.cos(angles)
    sine_part = jnp.sin(angles)
    return jnp.concatenate(
        (
            first_half * cosine - second_half * sine_part,
            second_half * cosine + first_half * sine_part,
        ),
        -1,
    )


def body(tokens, norm_gain, segments, deal_table, projection):
    group_id = lax.axis_index("dp")
    device_number = lax.axis_index("tensor")
    tensor_width = lax.axis_size("tensor")
    token_per_device = tokens.shape[1]
    model_width = tokens.shape[2]
    block_length = KEY_VALUE_HEADS * token_per_device
    head_number = device_number % KEY_VALUE_HEADS
    block_number = device_number // KEY_VALUE_HEADS
    group_queries = QUERY_HEADS // KEY_VALUE_HEADS
    head_bit_flags = KEY_VALUE_HEADS.bit_length() - 1
    level_bits = tensor_width.bit_length() - 1
    own_page = tokens[0]
    other_page = from_partner(own_page, "dp", 0)
    owner_group = jnp.sum(jnp.where(jnp.arange(deal_table.shape[1]) == group_id, deal_table[0], 0))
    stay_here = owner_group == group_id
    dealt_rows = jnp.where(stay_here, own_page, other_page)
    widened = dealt_rows.astype(jnp.float32)
    normed = (
        widened * lax.rsqrt(jnp.mean(widened * widened, -1, keepdims=True) + norm_eps) * norm_gain
    ).astype(jnp.bfloat16)
    segment_ids = segments[0]
    segment_match = segment_ids[:, None] == jnp.arange(NSEG)[None, :]
    counts_total = lax.psum(jnp.sum(segment_match.astype(jnp.float32), 0), "tensor")
    counts_int = counts_total.astype(jnp.int32)
    seg_starts = jnp.cumsum(counts_int) - counts_int
    row_starts = jnp.sum(jnp.where(segment_match, seg_starts[None, :], 0), 1)
    bit_order = list(range(head_bit_flags))
    rows_held = normed
    starts_held = row_starts
    gathered_bits = []
    for bit_index in bit_order:
        upper_flag = device_number >> bit_index & 1 == 1
        axis_pos = len([earlier for earlier in gathered_bits if earlier > bit_index])
        rows_far = from_partner(rows_held, "tensor", bit_index)
        starts_far = from_partner(starts_held, "tensor", bit_index)
        rows_held = stack_pair(rows_held, rows_far, upper_flag, axis_pos)
        starts_held = stack_pair(starts_held, starts_far, upper_flag, axis_pos)
        gathered_bits.append(bit_index)
    rows_block = rows_held.reshape(block_length, model_width)
    starts_block = starts_held.reshape(block_length)
    weights_held = projection
    for level_index in range(level_bits - head_bit_flags):
        bit_index = head_bit_flags + level_index
        upper_flag = device_number >> bit_index & 1 == 1
        arrived = from_partner(weights_held, "tensor", bit_index)
        weights_held = stack_pair(weights_held, arrived, upper_flag, 0).reshape(
            -1, weights_held.shape[1]
        )
    projected = jnp.dot(rows_block, weights_held, preferred_element_type=jnp.float32)
    rope_freq = rope_base ** (-(jnp.arange(0, HEAD_SIZE, 2).astype(jnp.float32) / HEAD_SIZE))
    block_positions = block_number * block_length + jnp.arange(block_length)
    angles = (block_positions - starts_block).astype(jnp.float32)[:, None] * rope_freq[None, :]
    queries = rotary(
        projected[:, : group_queries * HEAD_SIZE].reshape(block_length, group_queries, HEAD_SIZE),
        angles[:, None, :],
    ).astype(jnp.bfloat16)
    keys_own = rotary(
        projected[:, group_queries * HEAD_SIZE : (group_queries + 1) * HEAD_SIZE], angles
    ).astype(jnp.bfloat16)
    values_own = projected[:, (group_queries + 1) * HEAD_SIZE :].astype(jnp.bfloat16)
    local_pairs = jnp.concatenate((keys_own, values_own), 1)
    reach_blocks = -(-WINDOW // block_length)
    previous_pairs = [shifted(local_pairs, "tensor", 1 * KEY_VALUE_HEADS)]
    window_pairs = jnp.concatenate(previous_pairs + [local_pairs], 0)
    sink_positions = (seg_starts[:, None] + jnp.arange(SINKS)[None, :]).reshape(NSEG * SINKS)
    local_rows = sink_positions - block_number * block_length
    selector = (local_rows[:, None] == jnp.arange(block_length)[None, :]).astype(jnp.bfloat16)
    selected_rows = jnp.dot(selector, rows_block, preferred_element_type=jnp.float32)
    slice_width = model_width // KEY_VALUE_HEADS
    own_slice = jnp.arange(model_width) // slice_width == head_number
    slice_rows = jnp.where(own_slice[None, :], selected_rows, 0.0)
    sink_table = lax.psum(slice_rows, "tensor")
    sink_normed = sink_table.astype(jnp.bfloat16)
    sink_projected = jnp.dot(
        sink_normed,
        weights_held[:, group_queries * HEAD_SIZE :],
        preferred_element_type=jnp.float32,
    ).reshape(NSEG, SINKS, 2 * HEAD_SIZE)
    sink_angles = jnp.arange(SINKS).astype(jnp.float32)[:, None] * rope_freq[None, :]
    sink_key_rows = rotary(sink_projected[:, :, :HEAD_SIZE], sink_angles[None, :, :]).astype(
        jnp.bfloat16
    )
    sink_value_rows = sink_projected[:, :, HEAD_SIZE:].astype(jnp.bfloat16)
    sink_pairs = jnp.concatenate((sink_key_rows, sink_value_rows), -1)
    tile_rows = min(512, block_length)
    score_scale = HEAD_SIZE ** (-0.5)

    def attend(tile_start):
        query_tile = lax.dynamic_slice_in_dim(queries, tile_start, tile_rows, 0)
        query_pos = block_number * block_length + tile_start + jnp.arange(tile_rows)
        query_start = lax.dynamic_slice_in_dim(starts_block, tile_start, tile_rows, 0)
        key_from = reach_blocks * block_length + tile_start - WINDOW
        key_pairs = lax.dynamic_slice_in_dim(window_pairs, key_from, WINDOW + tile_rows, 0)
        key_pos = (
            (block_number - reach_blocks) * block_length + key_from + jnp.arange(WINDOW + tile_rows)
        )
        scores = (
            jnp.einsum(
                "rgd,kd->rgk",
                query_tile,
                key_pairs[:, :HEAD_SIZE],
                preferred_element_type=jnp.float32,
            )
            * score_scale
        )
        allowed = (
            (key_pos[None, :] <= query_pos[:, None])
            & (key_pos[None, :] >= query_start[:, None])
            & (key_pos[None, :] >= query_pos[:, None] - WINDOW)
        )
        chooser = (seg_starts[None, :] == query_start[:, None]).astype(jnp.bfloat16)
        row_sinks = jnp.einsum(
            "rs,sqc->rqc", chooser, sink_pairs, preferred_element_type=jnp.float32
        ).astype(jnp.bfloat16)
        sink_scores = (
            jnp.einsum(
                "rgd,rqd->rgq",
                query_tile,
                row_sinks[:, :, :HEAD_SIZE],
                preferred_element_type=jnp.float32,
            )
            * score_scale
        )
        sink_pos = query_start[:, None] + jnp.arange(SINKS)[None, :]
        sink_allowed = (sink_pos <= query_pos[:, None]) & (sink_pos < query_pos[:, None] - WINDOW)
        masked = jnp.where(allowed[:, None, :], scores, -jnp.inf)
        masked_sinks = jnp.where(sink_allowed[:, None, :], sink_scores, -jnp.inf)
        top_score = jnp.maximum(
            jnp.max(masked, -1, keepdims=True), jnp.max(masked_sinks, -1, keepdims=True)
        )
        window_weights = jnp.exp(masked - top_score)
        sink_weights = jnp.exp(masked_sinks - top_score)
        denominator = jnp.sum(window_weights, -1, keepdims=True) + jnp.sum(
            sink_weights, -1, keepdims=True
        )
        window_probs = (window_weights / denominator).astype(jnp.bfloat16)
        sink_probs = (sink_weights / denominator).astype(jnp.bfloat16)
        mixed_rows = jnp.einsum(
            "rgk,kd->rgd",
            window_probs,
            key_pairs[:, HEAD_SIZE:],
            preferred_element_type=jnp.float32,
        )
        mixed_rows = mixed_rows + jnp.einsum(
            "rgq,rqd->rgd",
            sink_probs,
            row_sinks[:, :, HEAD_SIZE:],
            preferred_element_type=jnp.float32,
        )
        return mixed_rows.astype(jnp.bfloat16).reshape(tile_rows, group_queries * HEAD_SIZE)

    tile_offsets = jnp.arange(block_length // tile_rows, dtype=jnp.int32) * tile_rows
    context_block = lax.map(attend, tile_offsets).reshape(block_length, group_queries * HEAD_SIZE)
    pairs_by_dest = local_pairs.reshape((2,) * head_bit_flags + (token_per_device, 2 * HEAD_SIZE))
    context_by_dest = context_block.reshape(
        (2,) * head_bit_flags + (token_per_device, group_queries * HEAD_SIZE)
    )
    kept_pairs = pairs_by_dest
    for bit_index in range(head_bit_flags):
        axis_pos = head_bit_flags - 1 - bit_index
        bit_value = device_number >> bit_index & 1
        own_half = lax.dynamic_index_in_dim(kept_pairs, bit_value, axis_pos, keepdims=False)
        sent_half = lax.dynamic_index_in_dim(kept_pairs, 1 - bit_value, axis_pos, keepdims=False)
        arrived = from_partner(sent_half, "tensor", bit_index)
        kept_pairs = stack_pair(own_half, arrived, bit_value == 1, axis_pos)
    kept_context = context_by_dest
    for bit_index in range(head_bit_flags):
        axis_pos = head_bit_flags - 1 - bit_index
        bit_value = device_number >> bit_index & 1
        own_half = lax.dynamic_index_in_dim(kept_context, bit_value, axis_pos, keepdims=False)
        sent_half = lax.dynamic_index_in_dim(kept_context, 1 - bit_value, axis_pos, keepdims=False)
        arrived = from_partner(sent_half, "tensor", bit_index)
        kept_context = stack_pair(own_half, arrived, bit_value == 1, axis_pos)
    cached_heads = kept_pairs.reshape(KEY_VALUE_HEADS, token_per_device, 2 * HEAD_SIZE)
    key_cache = cached_heads[:, :, :HEAD_SIZE][None]
    value_cache = cached_heads[:, :, HEAD_SIZE:][None]
    context_local = (
        kept_context.reshape(KEY_VALUE_HEADS, token_per_device, group_queries * HEAD_SIZE)
        .transpose(1, 0, 2)
        .reshape(token_per_device, QUERY_HEADS * HEAD_SIZE)
    )
    context_back = from_partner(context_local, "dp", 0)
    context = jnp.where(stay_here, context_local, context_back)[None]
    return (context, key_cache, value_cache)


def solution(mesh):
    placed = (P("dp", "tensor", None), P(), P("dp", "tensor"), P("tensor", None), P("tensor", None))
    return jax.shard_map(
        body,
        mesh=mesh,
        in_specs=placed,
        out_specs=(
            P("dp", "tensor", None),
            P("dp", None, "tensor", None),
            P("dp", None, "tensor", None),
        ),
        check_vma=False,
    )
```

profile of v0, /device:TPU:32, one launch (start us, length us, event | category | flops | bytes accessed | tf_op | source)
XLA Modules:
  0.0 1571.1 jit_solution(10747229112647004159)
XLA Ops:
  4.5 7.4 collective-permute-done.7
  16.3 9.5 collective-permute-done.3
  27.6 5.5 collective-permute-done.8
  43.6 25.5 %collective-permute-done.9 = bf16[1024,768]{1,0:T(8,128)(2,1)} collective-permute-done((bf16[1024,768]{1,0:T(8,128)(2,1)S(1)}, bf16[1024,768]{1,0:T(8,128)(2,1)}, u32[]{:S(2)}, u32[]{:S(2)}) %collective-permute-start.9) | collective-permute-done | bytes 1572896 | tf_op jit(solution)/shard_map/ppermute | solution.py:21
  75.8 56.0 %collective-permute-done.5 = bf16[2,128,4096]{2,1,0:T(8,128)(2,1)} collective-permute-done((bf16[2,128,4096]{2,1,0:T(8,128)(2,1)}, bf16[2,128,4096]{2,1,0:T(8,128)(2,1)}, u32[]{:S(2)}, u32[]{:S(2)}) %collective-permute-start.5) | collective-permute-done | bytes 2097184 | tf_op jit(solution)/shard_map/ppermute | solution.py:21
  136.4 4.6 collective-permute-start.6
  141.1 513.5 %psum.14 = f32[8]{0:T(128)S(1)} all-reduce(f32[8]{0:T(128)S(1)} %convert_reduce_fusion), channel_id=1, replica_groups=mesh['dp'=2,'tensor'=128] {'tensor'}, use_global_device_ids=true, to_apply=%region_3.4 | all-reduce | flops 8 | bytes 64 | tf_op jit(solution)/shard_map/psum | solution.py:74
  658.0 4.4 collective-permute-done.1
  663.4 6.9 collective-permute-done.2
  678.6 5.1 select_bitcast_fusion.1
  683.8 7.6 pad_maximum_fusion
  691.4 11.3 fusion.60
  705.0 684.3 %all-reduce.1 = bf16[32,4096]{1,0:T(8,128)(2,1)S(1)} all-reduce(f32[32,4096]{1,0:T(8,128)} %convolution_select_fusion), channel_id=1, replica_groups=mesh['dp'=2,'tensor'=128] {'tensor'}, use_global_device_ids=true, to_apply=%region_6.7 | all-reduce | flops 131072 | bytes 786432 | tf_op jit(solution)/shard_map/psum | solution.py:123
  1413.2 57.3 %while.15 = (s32[]{:T(128)}, bf16[2,512,512]{2,1,0:T(8,128)(2,1)}, s32[2]{0:T(128)}, s32[]{:T(128)}, s32[]{:T(128)}, /*index=5*/s32[1024]{0:T(1024)}, bf16[1024,...) while((s32[]{:T(128)}, bf16[2,512,512]{2,1,0:T(8,128)(2,1)}, ...), condition=%wide.region_12.13_spmd, body=%wide.region_7.12_spmd.sunk | while | flops 1115269120 | bytes 41343824 | solution.py:204
  1422.2 5.9 fusion.93
  1429.4 4.7 fusion.96
  1435.5 5.2 fusion.99
  1450.9 5.9 fusion.93
  1458.0 4.7 fusion.96
  1464.2 5.2 fusion.99
  1478.9 17.6 %collective-permute-done.13 = bf16[2,2,128,512]{3,2,1,0:T(8,128)(2,1)S(1)} collective-permute-done((bf16[2,2,128,512]{3,2,1,0:T(8,128)(2,1)S(1)}, bf16[2,2,128,512]{3,2,1,0:T(8,128)(2,1)S(1)}, u32[]{:S(2)}, u32[]{:S(2)}) %collective-permute-start.13) | collective-permute-done | bytes 524320 | tf_op jit(solution)/shard_map/ppermute | solution.py:21
  1502.3 19.0 %collective-permute-done.14 = bf16[2,2,128,512]{3,2,1,0:T(8,128)(2,1)S(1)} collective-permute-done((bf16[2,2,128,512]{3,2,1,0:T(8,128)(2,1)S(1)}, bf16[2,2,128,512]{3,2,1,0:T(8,128)(2,1)S(1)}, u32[]{:S(2)}, u32[]{:S(2)}) %collective-permute-start.14) | collective-permute-done | bytes 524320 | tf_op jit(solution)/shard_map/ppermute | solution.py:21
  1522.8 6.4 collective-permute-start.15
  1537.3 31.6 %collective-permute-done.18 = bf16[2,2,128,256]{3,2,1,0:T(8,128)(2,1)S(1)} collective-permute-done((bf16[2,2,128,256]{3,2,1,0:T(8,128)(2,1)S(1)}, bf16[2,2,128,256]{3,2,1,0:T(8,128)(2,1)S(1)}, u32[]{:S(2)}, u32[]{:S(2)}) %collective-permute-start.18) | collective-permute-done | bytes 262176 | tf_op jit(solution)/shard_map/ppermute | solution.py:21
  (175 shorter events, 113.7 us)
Async XLA Ops:
  0.6 25.2 %copy-start.7 = (bf16[1,128,4096]{2,1,0:T(8,128)(2,1)S(1)}, bf16[1,128,4096]{2,1,0:T(8,128)(2,1)}, u32[]{:S(2)}) copy-start(bf16[1,128,4096]{2,1,0:T(8,128)(2,1)} %param.7) | copy-start | bytes 3145732
  0.6 26.2 %copy-start.12 = (f32[4096]{0:T(1024)S(1)}, f32[4096]{0:T(1024)}, u32[]{:S(2)}) copy-start(f32[4096]{0:T(1024)} %param.8) | copy-start | bytes 49156
  0.7 25.2 %collective-permute-start.3 = (bf16[128,4096]{1,0:T(8,128)(2,1)}, bf16[128,4096]{1,0:T(8,128)(2,1)S(1)}, u32[]{:S(2)}, u32[]{:S(2)}) collective-permute-start(bf16[128,4096]{1,0:T(8,128)(2,1)} %bitcast.201), channel_id=1, source_target_pairs={{0,128},{128,0},{1,129},{129,1},{2,130},{130,2},{3,131},{131,3},{4... | collective-permute-start | bytes 3145736 | tf_op jit(solution)/shard_map/ppermute | solution.py:21
  2.6 9.3 collective-permute-start.7
  13.0 20.1 %collective-permute-start.8 = (bf16[512,768]{1,0:T(8,128)(2,1)S(1)}, bf16[512,768]{1,0:T(8,128)(2,1)}, u32[]{:S(2)}, u32[]{:S(2)}) collective-permute-start(bf16[512,768]{1,0:T(8,128)(2,1)S(1)} %bitcast.202), channel_id=1, source_target_pairs={{0,16},{1,17},{2,18},{3,19},{4,20},{5,21},{6,22},{7,23},{8,24},{9,... | collective-permute-start | bytes 2359304 | tf_op jit(solution)/shard_map/ppermute | solution.py:21
  27.3 8.9 collective-permute-start.4
  34.5 34.6 %collective-permute-start.9 = (bf16[1024,768]{1,0:T(8,128)(2,1)S(1)}, bf16[1024,768]{1,0:T(8,128)(2,1)}, u32[]{:S(2)}, u32[]{:S(2)}) collective-permute-start(bf16[1024,768]{1,0:T(8,128)(2,1)S(1)} %bitcast.198), channel_id=1, source_target_pairs={{0,32},{1,33},{2,34},{3,35},{4,36},{5,37},{6,38},{7,39},{8,40},{9,... | collective-permute-start | bytes 4718600 | tf_op jit(solution)/shard_map/ppermute | solution.py:21
  40.3 91.4 %collective-permute-start.5 = (bf16[2,128,4096]{2,1,0:T(8,128)(2,1)}, bf16[2,128,4096]{2,1,0:T(8,128)(2,1)}, u32[]{:S(2)}, u32[]{:S(2)}) collective-permute-start(bf16[2,128,4096]{2,1,0:T(8,128)(2,1)} %pad_maximum_fusion.4), channel_id=1, source_target_pairs={{0,2},{1,3},{2,0},{3,1},{4,6},{5,7},{6,4},{7,5},{8,10},{9,11},{10,... | collective-permute-start | bytes 6291464 | tf_op jit(solution)/shard_map/ppermute | solution.py:21
  70.7 61.1 %copy-start.4 = (bf16[1,128,4096]{2,1,0:T(8,128)(2,1)S(1)}, bf16[1,128,4096]{2,1,0:T(8,128)(2,1)}, u32[]{:S(2)}) copy-start(bf16[1,128,4096]{2,1,0:T(8,128)(2,1)} %copy-done.3) | copy-start | bytes 3145732
  72.6 599.5 %collective-permute-start.10 = (bf16[2048,768]{1,0:T(8,128)(2,1)}, bf16[2048,768]{1,0:T(8,128)(2,1)}, u32[]{:S(2)}, u32[]{:S(2)}) collective-permute-start(bf16[2048,768]{1,0:T(8,128)(2,1)} %bitcast.32), channel_id=1, source_target_pairs={{0,64},{1,65},{2,66},{3,67},{4,68},{5,69},{6,70},{7,71},{8,72},{9,... | collective-permute-start | bytes 9437192 | tf_op jit(solution)/shard_map/ppermute | solution.py:21
  136.4 542.2 %collective-permute-start.6 = (bf16[2,2,128,4096]{3,2,1,0:T(8,128)(2,1)}, bf16[2,2,128,4096]{3,2,1,0:T(8,128)(2,1)}, u32[]{:S(2)}, u32[]{:S(2)}) collective-permute-start(bf16[2,2,128,4096]{3,2,1,0:T(8,128)(2,1)} %pad_maximum_fusion.2), channel_id=1, source_target_pairs={{0,4},{1,5},{2,6},{3,7},{4,0},{5,1},{6,2},{7,3},{8,12},{9,13},{10,... | collective-permute-start | bytes 12582920 | tf_op jit(solution)/shard_map/ppermute | solution.py:21
  655.9 2.0 collective-permute-start
  657.9 4.6 collective-permute-start.1
  662.5 7.8 collective-permute-start.2
  691.4 11.3 copy-start
  705.0 687.0 %copy-start.9 = (f32[1024,768]{0,1:T(8,128)S(1)}, f32[1024,768]{0,1:T(8,128)}, u32[]{:S(2)}) copy-start(f32[1024,768]{0,1:T(8,128)} %fusion.60) | copy-start | bytes 9437188
  1396.4 14.7 collective-permute-start.11
  1471.5 2.0 collective-permute-start.12
  1474.8 21.7 %collective-permute-start.13 = (bf16[2,2,128,512]{3,2,1,0:T(8,128)(2,1)S(1)}, bf16[2,2,128,512]{3,2,1,0:T(8,128)(2,1)S(1)}, u32[]{:S(2)}, u32[]{:S(2)}) collective-permute-start(bf16[2,2,128,512]{3,2,1,0:T(8,128)(2,1)S(1)} %bitcast.206), channel_id=1, source_target_pairs={{0,2},{1,3},{2,0},{3,1},{4,6},{5,7},{6,4},{7,5},{8,10},{9,11},{10,... | collective-permute-start | bytes 1572872 | tf_op jit(solution)/shard_map/ppermute | solution.py:21
  1478.8 18.4 %collective-permute-start.16 = (bf16[2,2,128,256]{3,2,1,0:T(8,128)(2,1)}, bf16[2,2,128,256]{3,2,1,0:T(8,128)(2,1)}, u32[]{:S(2)}, u32[]{:S(2)}) collective-permute-start(bf16[2,2,128,256]{3,2,1,0:T(8,128)(2,1)} %bitcast.54), channel_id=1, source_target_pairs={{0,1},{1,0},{2,3},{3,2},{4,5},{5,4},{6,7},{7,6},{8,9},{9,8},{10,11... | collective-permute-start | bytes 786440 | tf_op jit(solution)/shard_map/ppermute | solution.py:21
  1496.6 24.7 %collective-permute-start.14 = (bf16[2,2,128,512]{3,2,1,0:T(8,128)(2,1)S(1)}, bf16[2,2,128,512]{3,2,1,0:T(8,128)(2,1)S(1)}, u32[]{:S(2)}, u32[]{:S(2)}) collective-permute-start(bf16[2,2,128,512]{3,2,1,0:T(8,128)(2,1)S(1)} %fusion.31), channel_id=1, source_target_pairs={{0,4},{1,5},{2,6},{3,7},{4,0},{5,1},{6,2},{7,3},{8,12},{9,13},{10,... | collective-permute-start | bytes 1572872 | tf_op jit(solution)/shard_map/ppermute | solution.py:21
  1499.0 34.4 %collective-permute-start.17 = (bf16[2,2,128,256]{3,2,1,0:T(8,128)(2,1)}, bf16[2,2,128,256]{3,2,1,0:T(8,128)(2,1)}, u32[]{:S(2)}, u32[]{:S(2)}) collective-permute-start(bf16[2,2,128,256]{3,2,1,0:T(8,128)(2,1)} %bitcast.175), channel_id=1, source_target_pairs={{0,2},{1,3},{2,0},{3,1},{4,6},{5,7},{6,4},{7,5},{8,10},{9,11},{10,... | collective-permute-start | bytes 786440 | tf_op jit(solution)/shard_map/ppermute | solution.py:21
  1522.8 47.2 %collective-permute-start.15 = (bf16[128,4096]{1,0:T(8,128)(2,1)S(1)}, bf16[128,4096]{1,0:T(8,128)(2,1)S(1)}, u32[]{:S(2)}, u32[]{:S(2)}) collective-permute-start(bf16[128,4096]{1,0:T(8,128)(2,1)S(1)} %copy.230), channel_id=1, source_target_pairs={{0,128},{128,0},{1,129},{129,1},{2,130},{130,2},{3,131},{131,3},{4... | collective-permute-start | bytes 3145736 | tf_op jit(solution)/shard_map/ppermute | solution.py:21
  1534.4 34.5 %collective-permute-start.18 = (bf16[2,2,128,256]{3,2,1,0:T(8,128)(2,1)S(1)}, bf16[2,2,128,256]{3,2,1,0:T(8,128)(2,1)S(1)}, u32[]{:S(2)}, u32[]{:S(2)}) collective-permute-start(bf16[2,2,128,256]{3,2,1,0:T(8,128)(2,1)S(1)} %fusion.41), channel_id=1, source_target_pairs={{0,4},{1,5},{2,6},{3,7},{4,0},{5,1},{6,2},{7,3},{8,12},{9,13},{10,... | collective-permute-start | bytes 786440 | tf_op jit(solution)/shard_map/ppermute | solution.py:21
  (10 other events, 35.7 us)
where the time goes:
time: 1570 us
  blocking collectives  1200 us (76%)
  waiting for transfers between devices  190 us (12%)
  other arithmetic  67.2 us (4%)
  matrix products  43.1 us (3%)
  starting transfers between devices  33.9 us (2%)
  local copies, waits for them, and re-layouts  29.9 us (2%)
    psum x1, blocking collectives, body(): sink_table = lax.psum(slice_rows, 'tensor')  684 us
    psum x1, blocking collectives, body(): lax.psum(jnp.sum(segment_match.astype(jnp.float32), 0), 'tensor')  513 us
    ppermute x18, waiting for transfers between devices, from_partner(): return lax.ppermute(value, axis, pairs)  190 us
    another operation x30, other arithmetic, stack_pair(): return jnp.stack((lower_part, upper_part), axis=axis_pos)  37.3 us
    ppermute x18, starting transfers between devices, from_partner(): return lax.ppermute(value, axis, pairs)  31.8 us
  transfers between devices with their start and end apart: 19, of which 12 were waited for; matrix products, arithmetic and copies ran while one was open for 3% of the time, Pallas kernels for 0%

commit v1 on v0

--- a/solution.py
+++ b/solution.py
@@ -55,7 +55,6 @@
     token_per_device = tokens.shape[1]
     model_width = tokens.shape[2]
     block_length = KEY_VALUE_HEADS * token_per_device
-    head_number = device_number % KEY_VALUE_HEADS
     block_number = device_number // KEY_VALUE_HEADS
     group_queries = QUERY_HEADS // KEY_VALUE_HEADS
     head_bit_flags = KEY_VALUE_HEADS.bit_length() - 1
@@ -70,14 +69,9 @@
         widened * lax.rsqrt(jnp.mean(widened * widened, -1, keepdims=True) + norm_eps) * norm_gain
     ).astype(jnp.bfloat16)
     segment_ids = segments[0]
-    segment_match = segment_ids[:, None] == jnp.arange(NSEG)[None, :]
-    counts_total = lax.psum(jnp.sum(segment_match.astype(jnp.float32), 0), "tensor")
-    counts_int = counts_total.astype(jnp.int32)
-    seg_starts = jnp.cumsum(counts_int) - counts_int
-    row_starts = jnp.sum(jnp.where(segment_match, seg_starts[None, :], 0), 1)
     bit_order = list(range(head_bit_flags))
     rows_held = normed
-    starts_held = row_starts
+    starts_held = segment_ids
     gathered_bits = []
     for bit_index in bit_order:
         upper_flag = device_number >> bit_index & 1 == 1
@@ -88,7 +82,13 @@
         starts_held = stack_pair(starts_held, starts_far, upper_flag, axis_pos)
         gathered_bits.append(bit_index)
     rows_block = rows_held.reshape(block_length, model_width)
-    starts_block = starts_held.reshape(block_length)
+    segments_block = starts_held.reshape(block_length)
+    segment_match = segments_block[:, None] == jnp.arange(NSEG)[None, :]
+    counts_int = jnp.sum(segment_match.astype(jnp.int32), 0)
+    for bit_index in range(head_bit_flags, level_bits):
+        counts_int = counts_int + from_partner(counts_int, "tensor", bit_index)
+    seg_starts = jnp.cumsum(counts_int) - counts_int
+    starts_block = jnp.sum(jnp.where(segment_match, seg_starts[None, :], 0), 1)
     weights_held = projection
     for level_index in range(level_bits - head_bit_flags):
         bit_index = head_bit_flags + level_index
@@ -116,23 +116,12 @@
     sink_positions = (seg_starts[:, None] + jnp.arange(SINKS)[None, :]).reshape(NSEG * SINKS)
     local_rows = sink_positions - block_number * block_length
     selector = (local_rows[:, None] == jnp.arange(block_length)[None, :]).astype(jnp.bfloat16)
-    selected_rows = jnp.dot(selector, rows_block, preferred_element_type=jnp.float32)
-    slice_width = model_width // KEY_VALUE_HEADS
-    own_slice = jnp.arange(model_width) // slice_width == head_number
-    slice_rows = jnp.where(own_slice[None, :], selected_rows, 0.0)
-    sink_table = lax.psum(slice_rows, "tensor")
-    sink_normed = sink_table.astype(jnp.bfloat16)
-    sink_projected = jnp.dot(
-        sink_normed,
-        weights_held[:, group_queries * HEAD_SIZE :],
-        preferred_element_type=jnp.float32,
-    ).reshape(NSEG, SINKS, 2 * HEAD_SIZE)
-    sink_angles = jnp.arange(SINKS).astype(jnp.float32)[:, None] * rope_freq[None, :]
-    sink_key_rows = rotary(sink_projected[:, :, :HEAD_SIZE], sink_angles[None, :, :]).astype(
+    sink_flat = jnp.dot(selector, local_pairs, preferred_element_type=jnp.float32).astype(
         jnp.bfloat16
     )
-    sink_value_rows = sink_projected[:, :, HEAD_SIZE:].astype(jnp.bfloat16)
-    sink_pairs = jnp.concatenate((sink_key_rows, sink_value_rows), -1)
+    for bit_index in range(head_bit_flags, level_bits):
+        sink_flat = sink_flat + from_partner(sink_flat, "tensor", bit_index)
+    sink_pairs = sink_flat.reshape(NSEG, SINKS, 2 * HEAD_SIZE)
     tile_rows = min(512, block_length)
     score_scale = HEAD_SIZE ** (-0.5)
 

time: 1570 us -> 571 us (0.36)
  blocking collectives: 1200 us -> 0 us
  waiting for transfers between devices: 190 us -> 369 us
  starting transfers between devices: 33.9 us -> 66.9 us
    psum x2 -> x0, blocking collectives: 1200 us -> none  [the longest x1 684 us: body(): sink_table = lax.psum(slice_rows, 'tensor')]
    ppermute x18 -> x26, waiting for transfers between devices: 190 us -> 369 us  [from_partner(): return lax.ppermute(value, axis, pairs)]
    ppermute x18 -> x26, starting transfers between devices: 31.8 us -> 63.7 us  [from_partner(): return lax.ppermute(value, axis, pairs)]
  transfers between devices with their start and end apart: 19 -> 27, of which waited for: 12 -> 19; matrix products, arithmetic and copies ran while one was open for 3% -> 9% of each run, Pallas kernels for 0% -> 0%
where the time goes in v1:
time: 571 us; the launch traced here: 562 us
  waiting for transfers between devices  369 us (65%)
  starting transfers between devices  66.9 us (12%)
  other arithmetic  56.2 us (10%)
  local copies, waits for them, and re-layouts  30.1 us (5%)
  matrix products  29.5 us (5%)
  loops' own time  8.14 us (1%)
    ppermute x26, waiting for transfers between devices, from_partner(): return lax.ppermute(value, axis, pairs)  369 us
    ppermute x26, starting transfers between devices, from_partner(): return lax.ppermute(value, axis, pairs)  63.7 us
    another operation x30, other arithmetic, stack_pair(): return jnp.stack((lower_part, upper_part), axis=axis_pos)  36.7 us
  transfers between devices with their start and end apart: 27, of which 19 were waited for; matrix products, arithmetic and copies ran while one was open for 9% of the time, Pallas kernels for 0%

profile of v1, /device:TPU:32, one launch (start us, length us, event | category | flops | bytes accessed | tf_op | source)
XLA Modules:
  0.0 561.5 jit_solution(9840094845429284601)
XLA Ops:
  4.5 7.4 %collective-permute-done.11 = bf16[256,768]{1,0:T(8,128)(2,1)S(1)} collective-permute-done((bf16[256,768]{1,0:T(8,128)(2,1)}, bf16[256,768]{1,0:T(8,128)(2,1)S(1)}, u32[]{:S(2)}, u32[]{:S(2)}) %collective-permute-start.11) | collective-permute-done | bytes 393248 | tf_op jit(solution)/shard_map/ppermute | solution.py:21
  13.0 3.3 collective-permute-start.12
  16.3 9.5 %collective-permute-done.7 = bf16[128,4096]{1,0:T(8,128)(2,1)S(1)} collective-permute-done((bf16[128,4096]{1,0:T(8,128)(2,1)}, bf16[128,4096]{1,0:T(8,128)(2,1)S(1)}, u32[]{:S(2)}, u32[]{:S(2)}) %collective-permute-start.7) | collective-permute-done | bytes 1048608 | tf_op jit(solution)/shard_map/ppermute | solution.py:21
  27.4 5.7 %collective-permute-done.12 = bf16[512,768]{1,0:T(8,128)(2,1)} collective-permute-done((bf16[512,768]{1,0:T(8,128)(2,1)S(1)}, bf16[512,768]{1,0:T(8,128)(2,1)}, u32[]{:S(2)}, u32[]{:S(2)}) %collective-permute-start.12) | collective-permute-done | bytes 786464 | tf_op jit(solution)/shard_map/ppermute | solution.py:21
  40.3 3.3 collective-permute-start.9
  43.6 25.5 %collective-permute-done.13 = bf16[1024,768]{1,0:T(8,128)(2,1)} collective-permute-done((bf16[1024,768]{1,0:T(8,128)(2,1)S(1)}, bf16[1024,768]{1,0:T(8,128)(2,1)}, u32[]{:S(2)}, u32[]{:S(2)}) %collective-permute-start.13) | collective-permute-done | bytes 1572896 | tf_op jit(solution)/shard_map/ppermute | solution.py:21
  75.7 56.0 %collective-permute-done.9 = bf16[2,128,4096]{2,1,0:T(8,128)(2,1)} collective-permute-done((bf16[2,128,4096]{2,1,0:T(8,128)(2,1)}, bf16[2,128,4096]{2,1,0:T(8,128)(2,1)}, u32[]{:S(2)}, u32[]{:S(2)}) %collective-permute-start.9) | collective-permute-done | bytes 2097184 | tf_op jit(solution)/shard_map/ppermute | solution.py:21
  136.4 4.6 collective-permute-start.10
  142.2 3.5 collective-permute-start.1
  145.6 177.3 %collective-permute-done.1 = s32[2,128]{1,0:T(2,128)S(1)} collective-permute-done((s32[2,128]{1,0:T(2,128)S(1)}, s32[2,128]{1,0:T(2,128)S(1)}, u32[]{:S(2)}, u32[]{:S(2)}) %collective-permute-start.1) | collective-permute-done | bytes 1056 | tf_op jit(solution)/shard_map/ppermute | solution.py:21
  326.1 4.5 collective-permute-done.2
  349.0 3.3 select_bitcast_fusion.3
  355.5 5.1 select_bitcast_fusion.1
  360.6 7.6 %pad_maximum_fusion = bf16[2,2,2,128,4096]{4,3,2,1,0:T(8,128)(2,1)} fusion(bf16[1,2,2,128,4096]{4,3,2,1,0:T(8,128)(2,1)} %get-tuple-element.352, bf16[1,2,2,128,4096]{4,3,2,1,0:T(8,128)(2,1)} %get-tuple-element.351), kind=kLoop, calls=%fused_computation.39 | loop fusion | flops 4194304 | bytes 16777216 | tf_op jit(solution)/shard_map/stack | solution.py:33
  368.2 9.2 %fusion.52 = f32[1024,768]{0,1:T(8,128)S(1)} fusion(bf16[1024,4096]{1,0:T(8,128)(2,1)} %bitcast.193, bf16[4096,768]{1,0:T(8,128)(2,1)S(1)} %bitcast.195), kind=kOutput, calls=%fused_computation.161 | convolution fusion | flops 6442450944 | bytes 17825792 | tf_op jit(solution)/shard_map/dot_general | solution.py:100
  411.0 44.8 %while.15 = (s32[]{:T(128)}, bf16[2,512,512]{2,1,0:T(8,128)(2,1)}, s32[2]{0:T(128)S(1)}, s32[]{:T(128)}, s32[]{:T(128)}, /*index=5*/s32[1024]{0:T(1024)S(1)}, bf...) while((s32[]{:T(128)}, bf16[2,512,512]{2,1,0:T(8,128)(2,1)}, ...), condition=%wide.region_10.11_spmd, body=%wide.region_5.10_spmd.sunk | while | flops 1115269120 | bytes 83286448 | solution.py:193
  426.9 5.3 fusion.90
  449.3 5.3 fusion.90
  463.3 20.3 %collective-permute-done.21 = bf16[2,2,128,512]{3,2,1,0:T(8,128)(2,1)S(1)} collective-permute-done((bf16[2,2,128,512]{3,2,1,0:T(8,128)(2,1)S(1)}, bf16[2,2,128,512]{3,2,1,0:T(8,128)(2,1)S(1)}, u32[]{:S(2)}, u32[]{:S(2)}) %collective-permute-start.21) | collective-permute-done | bytes 524320 | tf_op jit(solution)/shard_map/ppermute | solution.py:21
  489.0 3.4 collective-permute-start.25
  492.4 9.2 %collective-permute-done.22 = bf16[2,2,128,512]{3,2,1,0:T(8,128)(2,1)S(1)} collective-permute-done((bf16[2,2,128,512]{3,2,1,0:T(8,128)(2,1)S(1)}, bf16[2,2,128,512]{3,2,1,0:T(8,128)(2,1)S(1)}, u32[]{:S(2)}, u32[]{:S(2)}) %collective-permute-start.22) | collective-permute-done | bytes 524320 | tf_op jit(solution)/shard_map/ppermute | solution.py:21
  503.0 13.4 %collective-permute-start.23 = (bf16[128,4096]{1,0:T(8,128)(2,1)S(1)}, bf16[128,4096]{1,0:T(8,128)(2,1)S(1)}, u32[]{:S(2)}, u32[]{:S(2)}) collective-permute-start(bf16[128,4096]{1,0:T(8,128)(2,1)S(1)} %copy.212), channel_id=1, source_target_pairs={{0,128},{128,0},{1,129},{129,1},{2,130},{130,2},{3,131},{131,3},{4... | collective-permute-start | bytes 3145736 | tf_op jit(solution)/shard_map/ppermute | solution.py:21
  516.4 6.0 %collective-permute-done.25 = bf16[2,2,128,256]{3,2,1,0:T(8,128)(2,1)} collective-permute-done((bf16[2,2,128,256]{3,2,1,0:T(8,128)(2,1)}, bf16[2,2,128,256]{3,2,1,0:T(8,128)(2,1)}, u32[]{:S(2)}, u32[]{:S(2)}) %collective-permute-start.25) | collective-permute-done | bytes 262176 | tf_op jit(solution)/shard_map/ppermute | solution.py:21
  526.2 33.0 %collective-permute-done.26 = bf16[2,2,128,256]{3,2,1,0:T(8,128)(2,1)S(1)} collective-permute-done((bf16[2,2,128,256]{3,2,1,0:T(8,128)(2,1)S(1)}, bf16[2,2,128,256]{3,2,1,0:T(8,128)(2,1)S(1)}, u32[]{:S(2)}, u32[]{:S(2)}) %collective-permute-start.26) | collective-permute-done | bytes 262176 | tf_op jit(solution)/shard_map/ppermute | solution.py:21
  (200 shorter events, 129.9 us)
Async XLA Ops:
  0.7 25.2 %collective-permute-start.7 = (bf16[128,4096]{1,0:T(8,128)(2,1)}, bf16[128,4096]{1,0:T(8,128)(2,1)S(1)}, u32[]{:S(2)}, u32[]{:S(2)}) collective-permute-start(bf16[128,4096]{1,0:T(8,128)(2,1)} %bitcast.199), channel_id=1, source_target_pairs={{0,128},{128,0},{1,129},{129,1},{2,130},{130,2},{3,131},{131,3},{4... | collective-permute-start | bytes 3145736 | tf_op jit(solution)/shard_map/ppermute | solution.py:21
  2.6 9.3 %collective-permute-start.11 = (bf16[256,768]{1,0:T(8,128)(2,1)}, bf16[256,768]{1,0:T(8,128)(2,1)S(1)}, u32[]{:S(2)}, u32[]{:S(2)}) collective-permute-start(bf16[256,768]{1,0:T(8,128)(2,1)} %param.11), channel_id=1, source_target_pairs={{0,8},{1,9},{2,10},{3,11},{4,12},{5,13},{6,14},{7,15},{8,0},{9,1},... | collective-permute-start | bytes 1179656 | tf_op jit(solution)/shard_map/ppermute | solution.py:21
  13.0 20.1 %collective-permute-start.12 = (bf16[512,768]{1,0:T(8,128)(2,1)S(1)}, bf16[512,768]{1,0:T(8,128)(2,1)}, u32[]{:S(2)}, u32[]{:S(2)}) collective-permute-start(bf16[512,768]{1,0:T(8,128)(2,1)S(1)} %bitcast.200), channel_id=1, source_target_pairs={{0,16},{1,17},{2,18},{3,19},{4,20},{5,21},{6,22},{7,23},{8,24},{9,... | collective-permute-start | bytes 2359304 | tf_op jit(solution)/shard_map/ppermute | solution.py:21
  27.3 8.9 %collective-permute-start.8 = (bf16[128,4096]{1,0:T(8,128)(2,1)S(1)}, bf16[128,4096]{1,0:T(8,128)(2,1)}, u32[]{:S(2)}, u32[]{:S(2)}) collective-permute-start(bf16[128,4096]{1,0:T(8,128)(2,1)S(1)} %fusion.25), channel_id=1, source_target_pairs={{0,1},{1,0},{2,3},{3,2},{4,5},{5,4},{6,7},{7,6},{8,9},{9,8},{10,11... | collective-permute-start | bytes 3145736 | tf_op jit(solution)/shard_map/ppermute | solution.py:21
  34.5 34.6 %collective-permute-start.13 = (bf16[1024,768]{1,0:T(8,128)(2,1)S(1)}, bf16[1024,768]{1,0:T(8,128)(2,1)}, u32[]{:S(2)}, u32[]{:S(2)}) collective-permute-start(bf16[1024,768]{1,0:T(8,128)(2,1)S(1)} %bitcast.196), channel_id=1, source_target_pairs={{0,32},{1,33},{2,34},{3,35},{4,36},{5,37},{6,38},{7,39},{8,40},{9,... | collective-permute-start | bytes 4718600 | tf_op jit(solution)/shard_map/ppermute | solution.py:21
  40.3 91.4 %collective-permute-start.9 = (bf16[2,128,4096]{2,1,0:T(8,128)(2,1)}, bf16[2,128,4096]{2,1,0:T(8,128)(2,1)}, u32[]{:S(2)}, u32[]{:S(2)}) collective-permute-start(bf16[2,128,4096]{2,1,0:T(8,128)(2,1)} %pad_maximum_fusion.4), channel_id=1, source_target_pairs={{0,2},{1,3},{2,0},{3,1},{4,6},{5,7},{6,4},{7,5},{8,10},{9,11},{10,... | collective-permute-start | bytes 6291464 | tf_op jit(solution)/shard_map/ppermute | solution.py:21
  72.6 276.4 %collective-permute-start.14 = (bf16[2048,768]{1,0:T(8,128)(2,1)}, bf16[2048,768]{1,0:T(8,128)(2,1)}, u32[]{:S(2)}, u32[]{:S(2)}) collective-permute-start(bf16[2048,768]{1,0:T(8,128)(2,1)} %bitcast.32), channel_id=1, source_target_pairs={{0,64},{1,65},{2,66},{3,67},{4,68},{5,69},{6,70},{7,71},{8,72},{9,... | collective-permute-start | bytes 9437192 | tf_op jit(solution)/shard_map/ppermute | solution.py:21
  136.4 219.1 %collective-permute-start.10 = (bf16[2,2,128,4096]{3,2,1,0:T(8,128)(2,1)}, bf16[2,2,128,4096]{3,2,1,0:T(8,128)(2,1)}, u32[]{:S(2)}, u32[]{:S(2)}) collective-permute-start(bf16[2,2,128,4096]{3,2,1,0:T(8,128)(2,1)} %pad_maximum_fusion.2), channel_id=1, source_target_pairs={{0,4},{1,5},{2,6},{3,7},{4,0},{5,1},{6,2},{7,3},{8,12},{9,13},{10,... | collective-permute-start | bytes 12582920 | tf_op jit(solution)/shard_map/ppermute | solution.py:21
  142.2 180.8 %collective-permute-start.1 = (s32[2,128]{1,0:T(2,128)S(1)}, s32[2,128]{1,0:T(2,128)S(1)}, u32[]{:S(2)}, u32[]{:S(2)}) collective-permute-start(s32[2,128]{1,0:T(2,128)S(1)} %pad_add_fusion.2), channel_id=1, source_target_pairs={{0,2},{1,3},{2,0},{3,1},{4,6},{5,7},{6,4},{7,5},{8,10},{9,11},{10,... | collective-permute-start | bytes 3080 | tf_op jit(solution)/shard_map/ppermute | solution.py:21
  323.0 7.6 %collective-permute-start.2 = (s32[2,2,128]{2,1,0:T(2,128)S(1)}, s32[2,2,128]{2,1,0:T(2,128)S(1)}, u32[]{:S(2)}, u32[]{:S(2)}) collective-permute-start(s32[2,2,128]{2,1,0:T(2,128)S(1)} %pad_add_fusion.1), channel_id=1, source_target_pairs={{0,4},{1,5},{2,6},{3,7},{4,0},{5,1},{6,2},{7,3},{8,12},{9,13},{10,... | collective-permute-start | bytes 6152 | tf_op jit(solution)/shard_map/ppermute | solution.py:21
  330.7 3.6 collective-permute-start.3
  334.4 5.1 collective-permute-start.4
  343.0 5.5 collective-permute-start.6
  379.7 6.5 %collective-permute-start.16 = (bf16[32,256]{1,0:T(8,128)(2,1)S(1)}, bf16[32,256]{1,0:T(8,128)(2,1)S(1)}, u32[]{:S(2)}, u32[]{:S(2)}) collective-permute-start(bf16[32,256]{1,0:T(8,128)(2,1)S(1)} %convolution_convert_fusion.1), channel_id=1, source_target_pairs={{0,8},{1,9},{2,10},{3,11},{4,12},{5,13},{6,14},{7,15},{8,0},{9,1},... | collective-permute-start | bytes 49160 | tf_op jit(solution)/shard_map/ppermute | solution.py:21
  383.0 25.9 %collective-permute-start.15 = (bf16[1024,256]{0,1:T(8,128)(2,1)S(1)}, bf16[1024,256]{0,1:T(8,128)(2,1)}, u32[]{:S(2)}, u32[]{:S(2)}) collective-permute-start(bf16[1024,256]{0,1:T(8,128)(2,1)S(1)} %pad_maximum_fusion.9), channel_id=1, source_target_pairs={{0,8},{1,9},{2,10},{3,11},{4,12},{5,13},{6,14},{7,15},{8,16},{9,17... | collective-permute-start | bytes 1572872 | tf_op jit(solution)/shard_map/ppermute | solution.py:27
  386.8 12.0 %collective-permute-start.17 = (bf16[32,256]{1,0:T(8,128)(2,1)}, bf16[32,256]{1,0:T(8,128)(2,1)}, u32[]{:S(2)}, u32[]{:S(2)}) collective-permute-start(bf16[32,256]{1,0:T(8,128)(2,1)} %add.289), channel_id=1, source_target_pairs={{0,16},{1,17},{2,18},{3,19},{4,20},{5,21},{6,22},{7,23},{8,24},{9,... | collective-permute-start | bytes 49160 | tf_op jit(solution)/shard_map/ppermute | solution.py:21
  399.5 3.8 collective-permute-start.18
  403.3 5.5 collective-permute-start.19
  460.3 23.3 %collective-permute-start.21 = (bf16[2,2,128,512]{3,2,1,0:T(8,128)(2,1)S(1)}, bf16[2,2,128,512]{3,2,1,0:T(8,128)(2,1)S(1)}, u32[]{:S(2)}, u32[]{:S(2)}) collective-permute-start(bf16[2,2,128,512]{3,2,1,0:T(8,128)(2,1)S(1)} %bitcast.204), channel_id=1, source_target_pairs={{0,2},{1,3},{2,0},{3,1},{4,6},{5,7},{6,4},{7,5},{8,10},{9,11},{10,... | collective-permute-start | bytes 1572872 | tf_op jit(solution)/shard_map/ppermute | solution.py:21
  463.2 24.1 %collective-permute-start.24 = (bf16[2,2,128,256]{3,2,1,0:T(8,128)(2,1)}, bf16[2,2,128,256]{3,2,1,0:T(8,128)(2,1)}, u32[]{:S(2)}, u32[]{:S(2)}) collective-permute-start(bf16[2,2,128,256]{3,2,1,0:T(8,128)(2,1)} %bitcast.54), channel_id=1, source_target_pairs={{0,1},{1,0},{2,3},{3,2},{4,5},{5,4},{6,7},{7,6},{8,9},{9,8},{10,11... | collective-permute-start | bytes 786440 | tf_op jit(solution)/shard_map/ppermute | solution.py:21
  483.7 17.9 %collective-permute-start.22 = (bf16[2,2,128,512]{3,2,1,0:T(8,128)(2,1)S(1)}, bf16[2,2,128,512]{3,2,1,0:T(8,128)(2,1)S(1)}, u32[]{:S(2)}, u32[]{:S(2)}) collective-permute-start(bf16[2,2,128,512]{3,2,1,0:T(8,128)(2,1)S(1)} %fusion.29), channel_id=1, source_target_pairs={{0,4},{1,5},{2,6},{3,7},{4,0},{5,1},{6,2},{7,3},{8,12},{9,13},{10,... | collective-permute-start | bytes 1572872 | tf_op jit(solution)/shard_map/ppermute | solution.py:21
  489.0 33.3 %collective-permute-start.25 = (bf16[2,2,128,256]{3,2,1,0:T(8,128)(2,1)}, bf16[2,2,128,256]{3,2,1,0:T(8,128)(2,1)}, u32[]{:S(2)}, u32[]{:S(2)}) collective-permute-start(bf16[2,2,128,256]{3,2,1,0:T(8,128)(2,1)} %bitcast.175), channel_id=1, source_target_pairs={{0,2},{1,3},{2,0},{3,1},{4,6},{5,7},{6,4},{7,5},{8,10},{9,11},{10,... | collective-permute-start | bytes 786440 | tf_op jit(solution)/shard_map/ppermute | solution.py:21
  503.0 57.2 %collective-permute-start.23 = (bf16[128,4096]{1,0:T(8,128)(2,1)S(1)}, bf16[128,4096]{1,0:T(8,128)(2,1)S(1)}, u32[]{:S(2)}, u32[]{:S(2)}) collective-permute-start(bf16[128,4096]{1,0:T(8,128)(2,1)S(1)} %copy.212), channel_id=1, source_target_pairs={{0,128},{128,0},{1,129},{129,1},{2,130},{130,2},{3,131},{131,3},{4... | collective-permute-start | bytes 3145736 | tf_op jit(solution)/shard_map/ppermute | solution.py:21
  523.3 35.9 %collective-permute-start.26 = (bf16[2,2,128,256]{3,2,1,0:T(8,128)(2,1)S(1)}, bf16[2,2,128,256]{3,2,1,0:T(8,128)(2,1)S(1)}, u32[]{:S(2)}, u32[]{:S(2)}) collective-permute-start(bf16[2,2,128,256]{3,2,1,0:T(8,128)(2,1)S(1)} %fusion.39), channel_id=1, source_target_pairs={{0,4},{1,5},{2,6},{3,7},{4,0},{5,1},{6,2},{7,3},{8,12},{9,13},{10,... | collective-permute-start | bytes 786440 | tf_op jit(solution)/shard_map/ppermute | solution.py:21
  (24 other events, 204.5 us)

commit v2 on v1

--- a/solution.py
+++ b/solution.py
@@ -1,6 +1,8 @@
 import jax
 import jax.numpy as jnp
 from jax import lax
+from jax.experimental import pallas as pl
+from jax.experimental.pallas import tpu as pltpu
 from jax.sharding import PartitionSpec as P
 
 QUERY_HEADS = 32
@@ -48,6 +50,190 @@
     )
 
 
+def gather_kernel(page, slab, note, pages, weights, notes, send, recv, local):
+    dp = lax.axis_index("dp")
+    t = lax.axis_index("tensor")
+    core, zh = t % 2, (t // 2) % 4
+    y, x = (t // 8) % 4, t // 32
+    z = zh * 2 + dp
+    q = t % 8
+
+    def device(dx, dy, z_at, core_at):
+        z_at = z_at % 8
+        block = ((x + dx) % 4) * 4 + (y + dy) % 4
+        return (z_at % 2, (block * 4 + z_at // 2) * 2 + core_at)
+
+    slots = {}
+
+    def copy(key, src, dst, target):
+        i = slots.setdefault(key, len(slots))
+        return pltpu.make_async_remote_copy(
+            src_ref=src,
+            dst_ref=dst,
+            send_sem=send.at[i],
+            recv_sem=recv.at[i],
+            device_id=target,
+            device_id_type=pl.DeviceIdType.MESH,
+        )
+
+    started = []
+
+    def start(key, src, dst, target):
+        c = copy(key, src, dst, target)
+        c.start()
+        started.append(c)
+
+    partner = (dp, t + 1 - 2 * core)
+
+    def arrived(key, dst):
+        copy(key, dst, dst, partner).wait_recv()
+
+    group = [(dp, (t // 8) * 8 + (q + r) % 8) for r in range(1, 8)]
+    columns = [device(r, 0, z, core) for r in range(1, 4)]
+    lines = [device(0, r, z, core) for r in range(1, 4)]
+    ring = {1: device(0, 0, z + 1, core), -1: device(0, 0, z + 7, core)}
+    barrier = pltpu.get_barrier_semaphore()
+    peers = group + columns + lines + [ring[1], ring[-1]]
+    for peer in peers:
+        pl.semaphore_signal(barrier, inc=1, device_id=peer, device_id_type=pl.DeviceIdType.MESH)
+    pl.semaphore_wait(barrier, len(peers))
+
+    def page_at(dz, h, c):
+        return pages.at[(z + dz + 8) % 8, c, h]
+
+    def origin(order, da, db):
+        dx, dy = (da, db) if order == 0 else (db, da)
+        return weights.at[((x + dx + 4) % 4) * 4 + (y + dy + 4) % 4, order]
+
+    def towards(order, da, db):
+        dx, dy = (da, db) if order == 0 else (db, da)
+        return device(dx + 4, dy + 4, z, core)
+
+    own_copies = [
+        pltpu.make_async_copy(page, pages.at[z, core], local.at[0]),
+        pltpu.make_async_copy(slab, weights.at[x * 4 + y], local.at[1]),
+        pltpu.make_async_copy(note, notes.at[y, x, q], local.at[2]),
+    ]
+    for c in own_copies:
+        c.start()
+    for r in range(1, 8):
+        start(("note", r), note, notes.at[y, x, q], group[r - 1])
+    for order in range(2):
+        for d in (1, -1):
+            start(("w1", order, d), slab.at[order], origin(order, 0, 0), towards(order, d, 0))
+    for h in range(2):
+        for d in (1, -1):
+            start(("z", d, 0, h), page.at[h], page_at(0, h, core), ring[d])
+    for order in range(2):
+        for d in (1, -1):
+            start(("w2", order, 0, d), slab.at[order], origin(order, 0, 0), towards(order, 0, d))
+    for h in range(2):
+        start(("c", 0, 0, h), page.at[h], page_at(0, h, core), partner)
+
+    def page_step(s, h):
+        for d in (1, -1):
+            if s == 3 and h != (0 if d == 1 else 1):
+                continue
+            at = page_at(-d * (s + 1), h, core)
+            arrived(("z", d, s, h), at)
+            if s + 1 < 3 or (s + 1 == 3 and h == (0 if d == 1 else 1)):
+                start(("z", d, s + 1, h), at, at, ring[d])
+            start(("c", d, s, h), at, at, partner)
+
+    def second_send(order, k):
+        for d in (1, -1):
+            start(("w2", order, k, d), origin(order, k, 0), origin(order, k, 0), towards(order, 0, d))
+
+    def second_relay(order, k):
+        for d in (1, -1):
+            at = origin(order, k, -d)
+            arrived(("w2", order, k, d), at)
+            half = at.at[0 if d == 1 else 1]
+            start(("w2r", order, k, d), half, half, towards(order, 0, d))
+
+    for r in range(1, 8):
+        arrived(("note", r), notes.at[y, x, (q + 8 - r) % 8])
+    own_copies[2].wait()
+    for r in range(1, 4):
+        start(("notex", r), notes.at[y, x], notes.at[y, x], columns[r - 1])
+    for order in range(2):
+        for d in (1, -1):
+            at = origin(order, -d, 0)
+            arrived(("w1", order, d), at)
+            half = at.at[0 if d == 1 else 1]
+            start(("w1r", order, d), half, half, towards(order, d, 0))
+            second_send(order, -d)
+    for order in range(2):
+        second_relay(order, 0)
+    for r in range(1, 4):
+        arrived(("notex", r), notes.at[y, (x + 4 - r) % 4])
+    for r in range(1, 4):
+        start(("notey", r), notes.at[y], notes.at[y], lines[r - 1])
+    page_step(0, 0)
+    for order in range(2):
+        for d in (1, -1):
+            arrived(("w1r", order, d), origin(order, -2 * d, 0).at[0 if d == 1 else 1])
+        second_send(order, 2)
+    for order in range(2):
+        second_relay(order, -1)
+        second_relay(order, 1)
+    page_step(0, 1)
+    for order in range(2):
+        second_relay(order, 2)
+    page_step(1, 0)
+    for r in range(1, 4):
+        arrived(("notey", r), notes.at[(y + 4 - r) % 4])
+    for order in range(2):
+        for k in (0, -1, 1, 2):
+            for d in (1, -1):
+                arrived(("w2r", order, k, d), origin(order, k, -2 * d).at[0 if d == 1 else 1])
+    page_step(1, 1)
+    for s, h in ((2, 0), (2, 1), (3, 0), (3, 1)):
+        page_step(s, h)
+    for h in range(2):
+        arrived(("c", 0, 0, h), page_at(0, h, 1 - core))
+    for s in range(4):
+        for h in range(2):
+            for d in (1, -1):
+                if s < 3 or h == (0 if d == 1 else 1):
+                    arrived(("c", d, s, h), page_at(-d * (s + 1), h, 1 - core))
+    for c in started:
+        c.wait_send()
+    own_copies[0].wait()
+    own_copies[1].wait()
+
+
+COPIES = 7 + 3 + 3 + 14 + 16 + 4 + 4 + 16 + 16
+
+
+def gather(page, slab, note):
+    rows, width = page.shape
+    depth, columns = slab.shape
+    vmem = pl.BlockSpec(memory_space=pltpu.VMEM)
+    hbm = pl.BlockSpec(memory_space=pltpu.HBM)
+    return pl.pallas_call(
+        gather_kernel,
+        out_shape=(
+            jax.ShapeDtypeStruct((8, 2, 2, rows // 2, width), page.dtype),
+            jax.ShapeDtypeStruct((16, 2, 2, depth // 4, columns), slab.dtype),
+            jax.ShapeDtypeStruct((4, 4, 8, 1, note.shape[0]), note.dtype),
+        ),
+        in_specs=[vmem] * 3,
+        out_specs=(hbm,) * 3,
+        scratch_shapes=[
+            pltpu.SemaphoreType.DMA((COPIES,)),
+            pltpu.SemaphoreType.DMA((COPIES,)),
+            pltpu.SemaphoreType.DMA((3,)),
+        ],
+        compiler_params=pltpu.CompilerParams(collective_id=0, has_side_effects=True),
+        name="gather",
+    )(
+        page.reshape(2, rows // 2, width),
+        slab.reshape(2, 2, depth // 4, columns),
+        note.reshape(1, -1),
+    )
+
+
 def body(tokens, norm_gain, segments, deal_table, projection):
     group_id = lax.axis_index("dp")
     device_number = lax.axis_index("tensor")
@@ -60,43 +246,30 @@
     head_bit_flags = KEY_VALUE_HEADS.bit_length() - 1
     level_bits = tensor_width.bit_length() - 1
     own_page = tokens[0]
-    other_page = from_partner(own_page, "dp", 0)
     owner_group = jnp.sum(jnp.where(jnp.arange(deal_table.shape[1]) == group_id, deal_table[0], 0))
     stay_here = owner_group == group_id
-    dealt_rows = jnp.where(stay_here, own_page, other_page)
-    widened = dealt_rows.astype(jnp.float32)
+    widened = own_page.astype(jnp.float32)
     normed = (
         widened * lax.rsqrt(jnp.mean(widened * widened, -1, keepdims=True) + norm_eps) * norm_gain
     ).astype(jnp.bfloat16)
-    segment_ids = segments[0]
-    bit_order = list(range(head_bit_flags))
-    rows_held = normed
-    starts_held = segment_ids
-    gathered_bits = []
-    for bit_index in bit_order:
-        upper_flag = device_number >> bit_index & 1 == 1
-        axis_pos = len([earlier for earlier in gathered_bits if earlier > bit_index])
-        rows_far = from_partner(rows_held, "tensor", bit_index)
-        starts_far = from_partner(starts_held, "tensor", bit_index)
-        rows_held = stack_pair(rows_held, rows_far, upper_flag, axis_pos)
-        starts_held = stack_pair(starts_held, starts_far, upper_flag, axis_pos)
-        gathered_bits.append(bit_index)
-    rows_block = rows_held.reshape(block_length, model_width)
-    segments_block = starts_held.reshape(block_length)
-    segment_match = segments_block[:, None] == jnp.arange(NSEG)[None, :]
-    counts_int = jnp.sum(segment_match.astype(jnp.int32), 0)
-    for bit_index in range(head_bit_flags, level_bits):
-        counts_int = counts_int + from_partner(counts_int, "tensor", bit_index)
+    client = jnp.where(stay_here, group_id, 1 - group_id).astype(jnp.int32)
+    note = jnp.concatenate((segments[0], jnp.broadcast_to(client, segments[0].shape)))
+    pages, weights, notes = gather(normed, projection, note)
+    weights_held = weights.reshape(model_width, projection.shape[1])
+    notes = notes.reshape(4, 4, KEY_VALUE_HEADS, 2, token_per_device).transpose(1, 0, 2, 3, 4)
+    notes = notes.reshape(-1, KEY_VALUE_HEADS, 2, token_per_device)
+    counts_int = jnp.sum(
+        (notes[:, :, 0, :, None] == jnp.arange(NSEG)).astype(jnp.int32), (0, 1, 2)
+    )
     seg_starts = jnp.cumsum(counts_int) - counts_int
+    own_notes = lax.dynamic_index_in_dim(notes, block_number, 0, keepdims=False)
+    segment_match = own_notes[:, 0].reshape(block_length)[:, None] == jnp.arange(NSEG)[None, :]
     starts_block = jnp.sum(jnp.where(segment_match, seg_starts[None, :], 0), 1)
-    weights_held = projection
-    for level_index in range(level_bits - head_bit_flags):
-        bit_index = head_bit_flags + level_index
-        upper_flag = device_number >> bit_index & 1 == 1
-        arrived = from_partner(weights_held, "tensor", bit_index)
-        weights_held = stack_pair(weights_held, arrived, upper_flag, 0).reshape(
-            -1, weights_held.shape[1]
-        )
+    clients = own_notes[:, 1, 0].reshape(4, 2, 1, 1)
+    pages = pages.reshape(4, 2, 2, token_per_device, model_width)
+    rows_block = jnp.where(clients == 1, pages[:, 1], pages[:, 0]).reshape(
+        block_length, model_width
+    )
     projected = jnp.dot(rows_block, weights_held, preferred_element_type=jnp.float32)
     rope_freq = rope_base ** (-(jnp.arange(0, HEAD_SIZE, 2).astype(jnp.float32) / HEAD_SIZE))
     block_positions = block_number * block_length + jnp.arange(block_length)

time: 571 us -> 319 us (0.56); the launches traced: 562 us -> 317 us
  waiting for transfers between devices: 369 us -> 72.2 us
  Pallas kernels: 0 us -> 93.7 us
  starting transfers between devices: 66.9 us -> 37.6 us
  other arithmetic: 56.2 us -> 38.1 us
    ppermute x26 -> x11, waiting for transfers between devices: 369 us -> 72.2 us  [from_partner(): return lax.ppermute(value, axis, pairs)]
    pallas_call x0 -> x1, Pallas kernels: none -> 93.7 us  [gather(): pl.pallas_call(gather_kernel, out_shape=(jax.ShapeDtypeStruct((8, 2, 2, r...]
    another operation x30 -> x10, other arithmetic: 36.7 us -> 3.59 us  [stack_pair(): return jnp.stack((lower_part, upper_part), axis=axis_pos)]
    ppermute x26 -> x11, starting transfers between devices: 63.7 us -> 33.4 us  [from_partner(): return lax.ppermute(value, axis, pairs)]
    select_n x0 -> x1, other arithmetic: none -> 6.5 us  [body(): jnp.where(clients == 1, pages[:, 1], pages[:, 0])]
  transfers between devices with their start and end apart: 27 -> 12, of which waited for: 19 -> 9; matrix products, arithmetic and copies ran while one was open for 9% -> 7% of each run, Pallas kernels for 0% -> 0%
where the time goes in v2:
time: 319 us; the launch traced here: 317 us
  Pallas kernels  93.7 us (29%)
  waiting for transfers between devices  72.2 us (23%)
  other arithmetic  38.1 us (12%)
  starting transfers between devices  37.6 us (12%)
  matrix products  34.9 us (11%)
  local copies, waits for them, and re-layouts  30.5 us (10%)
  loops' own time  8.08 us (3%)
    pallas_call x1, Pallas kernels, gather(): pl.pallas_call(gather_kernel, out_shape=(jax.ShapeDtypeStruct((8, 2, 2, r...  93.7 us
    ppermute x11, waiting for transfers between devices, from_partner(): return lax.ppermute(value, axis, pairs)  72.2 us
    ppermute x11, starting transfers between devices, from_partner(): return lax.ppermute(value, axis, pairs)  33.4 us
    dot_general x2, matrix products, attend(): jnp.einsum('rgk,kd->rgd', window_probs, key_pairs[:, HEAD_SIZE:], preferr...  10.6 us
    dot_general x2, matrix products, attend(): jnp.einsum('rgd,kd->rgk', query_tile, key_pairs[:, :HEAD_SIZE], preferred...  9.77 us
    reduce_sum x2, other arithmetic, attend(): jnp.sum(window_weights, -1, keepdims=True)  9.32 us
    dot_general x1, matrix products, body(): jnp.dot(rows_block, weights_held, preferred_element_type=jnp.float32)  9.08 us
    another operation x1, loops' own time, body(): lax.map(attend, tile_offsets)  8.08 us
  transfers between devices with their start and end apart: 12, of which 9 were waited for; matrix products, arithmetic and copies ran while one was open for 7% of the time, Pallas kernels for 0%

profile of v2, /device:TPU:32, one launch (start us, length us, event | category | flops | bytes accessed | tf_op | source)
XLA Modules:
  0.0 316.8 jit_solution(8402162169047750131)
XLA Ops:
  5.4 2.5 multiply_convert_fusion.page
  8.0 93.7 %gather.1 = (bf16[8,2,2,64,4096]{4,3,2,1,0:T(8,128)(2,1)}, bf16[16,2,2,64,768]{4,3,2,1,0:T(8,128)(2,1)}, s32[4,4,8,1,256]{4,3,2,1,0:T(1,128)}) custom-call(bf16[2,64,4096]{2,1,0:T(8,128)(2,1)} %multiply_convert_fusion.page, bf16[2,2,64,768]{3,2,1,0:T(8,128)(2,1)} %bitcast.164, s32[1,256]{1,0:T(1,128)} %bitcast.168), custom_call_target="tpu_custom_call" | custom-call | tf_op jit(solution)/shard_map/gather/pallas_call | solution.py:214
  103.8 6.5 %slice_select_fusion = bf16[4,1,2,128,4096]{4,3,2,1,0:T(8,128)(2,1)S(1)} fusion(bf16[4,2,2,128,4096]{4,3,2,1,0:T(8,128)(2,1)} %bitcast.153, pred[4,2]{1,0:T(4,128)(4,1)S(1)} %eq.124), kind=kLoop, calls=%fused_computation.39 | loop fusion | flops 4194304 | bytes 25165832 | tf_op jit(solution)/shard_map/jit(_where)/select_n | solution.py:270
  110.3 9.1 %fusion.48 = f32[1024,768]{0,1:T(8,128)S(1)} fusion(bf16[1024,4096]{1,0:T(8,128)(2,1)S(1)} %bitcast.155, bf16[4096,768]{1,0:T(8,128)(2,1)} %bitcast.171), kind=kOutput, calls=%fused_computation.132 | convolution fusion | flops 6442450944 | bytes 17825792 | tf_op jit(solution)/shard_map/dot_general | solution.py:273
  122.9 4.3 %collective-permute-start = (bf16[1024,256]{0,1:T(8,128)(2,1)S(1)}, bf16[1024,256]{0,1:T(8,128)(2,1)}, u32[]{:S(2)}, u32[]{:S(2)}) collective-permute-start(bf16[1024,256]{0,1:T(8,128)(2,1)S(1)} %pad_maximum_fusion.2), channel_id=1, source_target_pairs={{0,8},{1,9},{2,10},{3,11},{4,12},{5,13},{6,14},{7,15},{8,16},{9,17... | collective-permute-start | bytes 1572872 | tf_op jit(solution)/shard_map/ppermute | solution.py:29
  135.2 3.2 %copy.204 = f32[1024,4,64]{2,0,1:T(8,128)} copy(f32[1024,4,64]{0,2,1:T(8,128)} %get-tuple-element.363) | data formatting | bytes 2097152
  139.3 2.9 collective-permute-start.2
  148.4 3.3 %collective-permute-start.4 = (bf16[32,256]{1,0:T(8,128)(2,1)S(1)}, bf16[32,256]{1,0:T(8,128)(2,1)S(1)}, u32[]{:S(2)}, u32[]{:S(2)}) collective-permute-start(bf16[32,256]{1,0:T(8,128)(2,1)S(1)} %add.283), channel_id=1, source_target_pairs={{0,64},{1,65},{2,66},{3,67},{4,68},{5,69},{6,70},{7,71},{8,72},{9,... | collective-permute-start | bytes 49160 | tf_op jit(solution)/shard_map/ppermute | solution.py:23
  155.1 55.5 %while.15 = (s32[]{:T(128)}, bf16[2,512,512]{2,1,0:T(8,128)(2,1)}, s32[2]{0:T(128)}, s32[]{:T(128)}, s32[]{:T(128)}, /*index=5*/s32[1024]{0:T(1024)}, bf16[1024,...) while((s32[]{:T(128)}, bf16[2,512,512]{2,1,0:T(8,128)(2,1)}, ...), condition=%wide.region_10.11_spmd, body=%wide.region_5.10_spmd.sunk | while | flops 1115269120 | bytes 49732488 | solution.py:366
  164.2 4.9 %fusion.80 = (f32[512,4]{0,1:T(4,128)S(1)}, f32[512,4,1024]{2,0,1:T(8,128)}) fusion(pred[512,1024]{1,0:T(8,128)(4,1)S(1)} %compare_and_fusion.2, bf16[512,4,128]{2,0,1:T(8,128)(2,1)S(1)} %get-tuple-element.456, bf16[2048,256]{0,1:T(8,128)(2,1)S(1)} %get-tuple-element.501, s32[]{:T(128)S(6)} %select_n.291), kind=kOutput, calls=%fused_computation.3.clone.1 | convolution fusion | flops 543160320 | bytes 9707524 | tf_op jit(solution)/shard_map/while/body/eval_jaxpr/rgd,kd->rgk/dot_general | solution.py:311
  170.4 4.7 %fusion.83 = f32[512,4]{0,1:T(4,128)S(1)} fusion(f32[512,4,1024]{2,0,1:T(8,128)} %get-tuple-element.459, f32[512,4]{0,1:T(4,128)S(1)} %max.16, pred[512,1024]{1,0:T(8,128)(4,1)S(1)} %compare_and_fusion.2), kind=kLoop, calls=%fused_computation.4.clone.1 | loop fusion | flops 8386560 | bytes 8929280 | tf_op jit(solution)/shard_map/while/body/eval_jaxpr/reduce_sum | solution.py:346
  176.5 5.3 %fusion.86 = bf16[512,4,128]{0,2,1:T(8,128)(2,1)S(1)} fusion(f32[512,4,128]{0,2,1:T(8,128)S(1)} %copy.235, f32[512,4,1024]{2,0,1:T(8,128)} %get-tuple-element.459, f32[512,4]{0,1:T(4,128)S(1)} %add.360, f32[512,4]{0,1:T(4,128)S(1)} %max.16, pred[512,1024]{1,0:T(8,128)(4,1)S(1)} %compare_and_fusion.2, bf16[2048,256]{0,1:T(8,128)(2,1)} %copy-done, ...), kind=kOutput, calls=%fused_computation.9.clone.1 | convolution fusion | flops 547880960 | bytes 10764296 | tf_op jit(solution)/shard_map/while/body/eval_jaxpr/rgk,kd->rgd/dot_general | solution.py:351
  191.9 4.9 %fusion.80 = (f32[512,4]{0,1:T(4,128)S(1)}, f32[512,4,1024]{2,0,1:T(8,128)}) fusion(pred[512,1024]{1,0:T(8,128)(4,1)S(1)} %compare_and_fusion.2, bf16[512,4,128]{2,0,1:T(8,128)(2,1)S(1)} %get-tuple-element.456, bf16[2048,256]{0,1:T(8,128)(2,1)S(1)} %get-tuple-element.501, s32[]{:T(128)S(6)} %select_n.291), kind=kOutput, calls=%fused_computation.3.clone.1 | convolution fusion | flops 543160320 | bytes 9707524 | tf_op jit(solution)/shard_map/while/body/eval_jaxpr/rgd,kd->rgk/dot_general | solution.py:311
  198.1 4.7 %fusion.83 = f32[512,4]{0,1:T(4,128)S(1)} fusion(f32[512,4,1024]{2,0,1:T(8,128)} %get-tuple-element.459, f32[512,4]{0,1:T(4,128)S(1)} %max.16, pred[512,1024]{1,0:T(8,128)(4,1)S(1)} %compare_and_fusion.2), kind=kLoop, calls=%fused_computation.4.clone.1 | loop fusion | flops 8386560 | bytes 8929280 | tf_op jit(solution)/shard_map/while/body/eval_jaxpr/reduce_sum | solution.py:346
  204.2 5.3 %fusion.86 = bf16[512,4,128]{0,2,1:T(8,128)(2,1)S(1)} fusion(f32[512,4,128]{0,2,1:T(8,128)S(1)} %copy.235, f32[512,4,1024]{2,0,1:T(8,128)} %get-tuple-element.459, f32[512,4]{0,1:T(4,128)S(1)} %add.360, f32[512,4]{0,1:T(4,128)S(1)} %max.16, pred[512,1024]{1,0:T(8,128)(4,1)S(1)} %compare_and_fusion.2, bf16[2048,256]{0,1:T(8,128)(2,1)} %copy-done, ...), kind=kOutput, calls=%fused_computation.9.clone.1 | convolution fusion | flops 547880960 | bytes 10764296 | tf_op jit(solution)/shard_map/while/body/eval_jaxpr/rgk,kd->rgd/dot_general | solution.py:351
  215.0 2.8 collective-permute-start.6
  220.4 19.3 %collective-permute-done.6 = bf16[2,2,128,512]{3,2,1,0:T(8,128)(2,1)S(1)} collective-permute-done((bf16[2,2,128,512]{3,2,1,0:T(8,128)(2,1)S(1)}, bf16[2,2,128,512]{3,2,1,0:T(8,128)(2,1)S(1)}, u32[]{:S(2)}, u32[]{:S(2)}) %collective-permute-start.6) | collective-permute-done | bytes 524320 | tf_op jit(solution)/shard_map/ppermute | solution.py:23
  239.9 3.2 %collective-permute-start.7 = (bf16[2,2,128,512]{3,2,1,0:T(8,128)(2,1)S(1)}, bf16[2,2,128,512]{3,2,1,0:T(8,128)(2,1)S(1)}, u32[]{:S(2)}, u32[]{:S(2)}) collective-permute-start(bf16[2,2,128,512]{3,2,1,0:T(8,128)(2,1)S(1)} %fusion.26), channel_id=1, source_target_pairs={{0,4},{1,5},{2,6},{3,7},{4,0},{5,1},{6,2},{7,3},{8,12},{9,13},{10,... | collective-permute-start | bytes 1572872 | tf_op jit(solution)/shard_map/ppermute | solution.py:23
  245.4 3.4 %collective-permute-start.10 = (bf16[2,2,128,256]{3,2,1,0:T(8,128)(2,1)}, bf16[2,2,128,256]{3,2,1,0:T(8,128)(2,1)}, u32[]{:S(2)}, u32[]{:S(2)}) collective-permute-start(bf16[2,2,128,256]{3,2,1,0:T(8,128)(2,1)} %bitcast.136), channel_id=1, source_target_pairs={{0,2},{1,3},{2,0},{3,1},{4,6},{5,7},{6,4},{7,5},{8,10},{9,11},{10,... | collective-permute-start | bytes 786440 | tf_op jit(solution)/shard_map/ppermute | solution.py:23
  248.7 9.6 %collective-permute-done.7 = bf16[2,2,128,512]{3,2,1,0:T(8,128)(2,1)S(1)} collective-permute-done((bf16[2,2,128,512]{3,2,1,0:T(8,128)(2,1)S(1)}, bf16[2,2,128,512]{3,2,1,0:T(8,128)(2,1)S(1)}, u32[]{:S(2)}, u32[]{:S(2)}) %collective-permute-start.7) | collective-permute-done | bytes 524320 | tf_op jit(solution)/shard_map/ppermute | solution.py:23
  259.1 12.4 %collective-permute-start.8 = (bf16[128,4096]{0,1:T(8,128)(2,1)S(1)}, bf16[128,4096]{0,1:T(8,128)(2,1)S(1)}, u32[]{:S(2)}, u32[]{:S(2)}) collective-permute-start(bf16[128,4096]{0,1:T(8,128)(2,1)S(1)} %bitcast.157), channel_id=1, source_target_pairs={{0,128},{128,0},{1,129},{129,1},{2,130},{130,2},{3,131},{131,3},{4... | collective-permute-start | bytes 3145736 | tf_op jit(solution)/shard_map/ppermute | solution.py:23
  271.6 6.4 %collective-permute-done.10 = bf16[2,2,128,256]{3,2,1,0:T(8,128)(2,1)} collective-permute-done((bf16[2,2,128,256]{3,2,1,0:T(8,128)(2,1)}, bf16[2,2,128,256]{3,2,1,0:T(8,128)(2,1)}, u32[]{:S(2)}, u32[]{:S(2)}) %collective-permute-start.10) | collective-permute-done | bytes 262176 | tf_op jit(solution)/shard_map/ppermute | solution.py:23
  279.0 2.9 collective-permute-start.11
  281.9 32.4 %collective-permute-done.11 = bf16[2,2,128,256]{3,2,1,0:T(8,128)(2,1)S(1)} collective-permute-done((bf16[2,2,128,256]{3,2,1,0:T(8,128)(2,1)S(1)}, bf16[2,2,128,256]{3,2,1,0:T(8,128)(2,1)S(1)}, u32[]{:S(2)}, u32[]{:S(2)}) %collective-permute-start.11) | collective-permute-done | bytes 262176 | tf_op jit(solution)/shard_map/ppermute | solution.py:23
  (132 shorter events, 59.5 us)
Async XLA Ops:
  119.4 3.5 %copy-start.4 = (f32[1024,768]{0,1:T(8,128)}, f32[1024,768]{0,1:T(8,128)S(1)}, u32[]{:S(2)}) copy-start(f32[1024,768]{0,1:T(8,128)S(1)} %fusion.48) | copy-start | bytes 9437188
  122.8 9.3 %copy-start.5 = (bf16[1024,64]{0,1:T(8,128)(2,1)}, bf16[1024,64]{0,1:T(8,128)(2,1)S(1)}, u32[]{:S(2)}) copy-start(bf16[1024,64]{0,1:T(8,128)(2,1)S(1)} %get-tuple-element.362) | copy-start | bytes 393220
  122.9 9.3 %copy-start.2 = (bf16[1024,256]{0,1:T(8,128)(2,1)}, bf16[1024,256]{0,1:T(8,128)(2,1)S(1)}, u32[]{:S(2)}) copy-start(bf16[1024,256]{0,1:T(8,128)(2,1)S(1)} %pad_maximum_fusion.2) | copy-start | bytes 1572868
  122.9 31.0 %collective-permute-start = (bf16[1024,256]{0,1:T(8,128)(2,1)S(1)}, bf16[1024,256]{0,1:T(8,128)(2,1)}, u32[]{:S(2)}, u32[]{:S(2)}) collective-permute-start(bf16[1024,256]{0,1:T(8,128)(2,1)S(1)} %pad_maximum_fusion.2), channel_id=1, source_target_pairs={{0,8},{1,9},{2,10},{3,11},{4,12},{5,13},{6,14},{7,15},{8,16},{9,17... | collective-permute-start | bytes 1572872 | tf_op jit(solution)/shard_map/ppermute | solution.py:29
  128.2 10.4 %collective-permute-start.1 = (bf16[32,256]{1,0:T(8,128)(2,1)S(1)}, bf16[32,256]{1,0:T(8,128)(2,1)}, u32[]{:S(2)}, u32[]{:S(2)}) collective-permute-start(bf16[32,256]{1,0:T(8,128)(2,1)S(1)} %convolution_convert_fusion.1), channel_id=1, source_target_pairs={{0,8},{1,9},{2,10},{3,11},{4,12},{5,13},{6,14},{7,15},{8,0},{9,1},... | collective-permute-start | bytes 49160 | tf_op jit(solution)/shard_map/ppermute | solution.py:23
  139.3 5.2 %collective-permute-start.2 = (bf16[32,256]{1,0:T(8,128)(2,1)S(1)}, bf16[32,256]{1,0:T(8,128)(2,1)S(1)}, u32[]{:S(2)}, u32[]{:S(2)}) collective-permute-start(bf16[32,256]{1,0:T(8,128)(2,1)S(1)} %add.281), channel_id=1, source_target_pairs={{0,16},{1,17},{2,18},{3,19},{4,20},{5,21},{6,22},{7,23},{8,24},{9,... | collective-permute-start | bytes 49160 | tf_op jit(solution)/shard_map/ppermute | solution.py:23
  144.4 9.5 %copy-start.6 = (bf16[1024,64]{0,1:T(8,128)(2,1)S(1)}, bf16[1024,64]{0,1:T(8,128)(2,1)}, u32[]{:S(2)}) copy-start(bf16[1024,64]{0,1:T(8,128)(2,1)} %copy-done.5) | copy-start | bytes 393220
  144.6 3.8 %collective-permute-start.3 = (bf16[32,256]{1,0:T(8,128)(2,1)S(1)}, bf16[32,256]{1,0:T(8,128)(2,1)S(1)}, u32[]{:S(2)}, u32[]{:S(2)}) collective-permute-start(bf16[32,256]{1,0:T(8,128)(2,1)S(1)} %add.282), channel_id=1, source_target_pairs={{0,32},{1,33},{2,34},{3,35},{4,36},{5,37},{6,38},{7,39},{8,40},{9,... | collective-permute-start | bytes 49160 | tf_op jit(solution)/shard_map/ppermute | solution.py:23
  148.4 5.5 %collective-permute-start.4 = (bf16[32,256]{1,0:T(8,128)(2,1)S(1)}, bf16[32,256]{1,0:T(8,128)(2,1)S(1)}, u32[]{:S(2)}, u32[]{:S(2)}) collective-permute-start(bf16[32,256]{1,0:T(8,128)(2,1)S(1)} %add.283), channel_id=1, source_target_pairs={{0,64},{1,65},{2,66},{3,67},{4,68},{5,69},{6,70},{7,71},{8,72},{9,... | collective-permute-start | bytes 49160 | tf_op jit(solution)/shard_map/ppermute | solution.py:23
  155.1 14.0 %copy-start = (bf16[2048,256]{0,1:T(8,128)(2,1)}, bf16[2048,256]{0,1:T(8,128)(2,1)S(1)}, u32[]{:S(2)}) copy-start(bf16[2048,256]{0,1:T(8,128)(2,1)S(1)} %get-tuple-element.501) | copy-start | bytes 3145732 | tf_op jit(solution)/shard_map/while
  176.5 6.4 %copy-start.1 = (bf16[2048,256]{0,1:T(8,128)(2,1)S(1)}, bf16[2048,256]{0,1:T(8,128)(2,1)}, u32[]{:S(2)}) copy-start(bf16[2048,256]{0,1:T(8,128)(2,1)} %copy-done) | copy-start | bytes 3145732 | tf_op jit(solution)/shard_map/while
  182.9 13.9 %copy-start = (bf16[2048,256]{0,1:T(8,128)(2,1)}, bf16[2048,256]{0,1:T(8,128)(2,1)S(1)}, u32[]{:S(2)}) copy-start(bf16[2048,256]{0,1:T(8,128)(2,1)S(1)} %get-tuple-element.501) | copy-start | bytes 3145732 | tf_op jit(solution)/shard_map/while
  204.2 6.4 %copy-start.1 = (bf16[2048,256]{0,1:T(8,128)(2,1)S(1)}, bf16[2048,256]{0,1:T(8,128)(2,1)}, u32[]{:S(2)}) copy-start(bf16[2048,256]{0,1:T(8,128)(2,1)} %copy-done) | copy-start | bytes 3145732 | tf_op jit(solution)/shard_map/while
  210.6 7.2 %copy-start.3 = (bf16[1024,256]{0,1:T(8,128)(2,1)S(1)}, bf16[1024,256]{0,1:T(8,128)(2,1)}, u32[]{:S(2)}) copy-start(bf16[1024,256]{0,1:T(8,128)(2,1)} %copy-done.2) | copy-start | bytes 1572868
  211.8 2.0 collective-permute-start.5
  215.0 24.7 %collective-permute-start.6 = (bf16[2,2,128,512]{3,2,1,0:T(8,128)(2,1)S(1)}, bf16[2,2,128,512]{3,2,1,0:T(8,128)(2,1)S(1)}, u32[]{:S(2)}, u32[]{:S(2)}) collective-permute-start(bf16[2,2,128,512]{3,2,1,0:T(8,128)(2,1)S(1)} %bitcast.163), channel_id=1, source_target_pairs={{0,2},{1,3},{2,0},{3,1},{4,6},{5,7},{6,4},{7,5},{8,10},{9,11},{10,... | collective-permute-start | bytes 1572872 | tf_op jit(solution)/shard_map/ppermute | solution.py:23
  220.4 23.2 %collective-permute-start.9 = (bf16[2,2,128,256]{3,2,1,0:T(8,128)(2,1)}, bf16[2,2,128,256]{3,2,1,0:T(8,128)(2,1)}, u32[]{:S(2)}, u32[]{:S(2)}) collective-permute-start(bf16[2,2,128,256]{3,2,1,0:T(8,128)(2,1)} %bitcast.40), channel_id=1, source_target_pairs={{0,1},{1,0},{2,3},{3,2},{4,5},{5,4},{6,7},{7,6},{8,9},{9,8},{10,11... | collective-permute-start | bytes 786440 | tf_op jit(solution)/shard_map/ppermute | solution.py:23
  239.9 18.4 %collective-permute-start.7 = (bf16[2,2,128,512]{3,2,1,0:T(8,128)(2,1)S(1)}, bf16[2,2,128,512]{3,2,1,0:T(8,128)(2,1)S(1)}, u32[]{:S(2)}, u32[]{:S(2)}) collective-permute-start(bf16[2,2,128,512]{3,2,1,0:T(8,128)(2,1)S(1)} %fusion.26), channel_id=1, source_target_pairs={{0,4},{1,5},{2,6},{3,7},{4,0},{5,1},{6,2},{7,3},{8,12},{9,13},{10,... | collective-permute-start | bytes 1572872 | tf_op jit(solution)/shard_map/ppermute | solution.py:23
  245.4 32.6 %collective-permute-start.10 = (bf16[2,2,128,256]{3,2,1,0:T(8,128)(2,1)}, bf16[2,2,128,256]{3,2,1,0:T(8,128)(2,1)}, u32[]{:S(2)}, u32[]{:S(2)}) collective-permute-start(bf16[2,2,128,256]{3,2,1,0:T(8,128)(2,1)} %bitcast.136), channel_id=1, source_target_pairs={{0,2},{1,3},{2,0},{3,1},{4,6},{5,7},{6,4},{7,5},{8,10},{9,11},{10,... | collective-permute-start | bytes 786440 | tf_op jit(solution)/shard_map/ppermute | solution.py:23
  259.1 56.2 %collective-permute-start.8 = (bf16[128,4096]{0,1:T(8,128)(2,1)S(1)}, bf16[128,4096]{0,1:T(8,128)(2,1)S(1)}, u32[]{:S(2)}, u32[]{:S(2)}) collective-permute-start(bf16[128,4096]{0,1:T(8,128)(2,1)S(1)} %bitcast.157), channel_id=1, source_target_pairs={{0,128},{128,0},{1,129},{129,1},{2,130},{130,2},{3,131},{131,3},{4... | collective-permute-start | bytes 3145736 | tf_op jit(solution)/shard_map/ppermute | solution.py:23
  279.0 35.3 %collective-permute-start.11 = (bf16[2,2,128,256]{3,2,1,0:T(8,128)(2,1)S(1)}, bf16[2,2,128,256]{3,2,1,0:T(8,128)(2,1)S(1)}, u32[]{:S(2)}, u32[]{:S(2)}) collective-permute-start(bf16[2,2,128,256]{3,2,1,0:T(8,128)(2,1)S(1)} %fusion.36), channel_id=1, source_target_pairs={{0,4},{1,5},{2,6},{3,7},{4,0},{5,1},{6,2},{7,3},{8,12},{9,13},{10,... | collective-permute-start | bytes 786440 | tf_op jit(solution)/shard_map/ppermute | solution.py:23

commit v3 on v2

--- a/solution.py
+++ b/solution.py
@@ -15,24 +15,6 @@
 
 rope_base = 500000.0
 norm_eps = 1e-05
-
-
-def from_partner(value, axis, apart):
-    mask = 2**apart
-    pairs = [(source, source ^ mask) for source in range(lax.axis_size(axis))]
-    return lax.ppermute(value, axis, pairs)
-
-
-def shifted(block, axis, distance):
-    devices = range(lax.axis_size(axis))
-    route = [(i - distance, i) for i in devices if i - distance in devices]
-    return lax.ppermute(block, axis, route)
-
-
-def stack_pair(holding, arrived, upper_flag, axis_pos):
-    lower_part = jnp.where(upper_flag, arrived, holding)
-    upper_part = jnp.where(upper_flag, holding, arrived)
-    return jnp.stack((lower_part, upper_part), axis=axis_pos)
 
 
 def rotary(values, angles):
@@ -234,17 +216,241 @@
     )
 
 
+PAGE_ROWS = 128
+REACH = WINDOW + PAGE_ROWS
+CONTEXT_COPIES = 16
+ATTEND_COPIES = CONTEXT_COPIES + 14 + 2 + 15
+
+
+def attend_kernel(
+    queries,
+    keys,
+    values,
+    starts,
+    sink_rows,
+    sink_pairs,
+    context,
+    key_out,
+    value_out,
+    key_window,
+    value_window,
+    sinks,
+    mixed,
+    send,
+    recv,
+    local,
+):
+    dp = lax.axis_index("dp")
+    t = lax.axis_index("tensor")
+    core, zh = t % 2, (t // 2) % 4
+    q, block = t % 8, t // 8
+    width = mixed.shape[2]
+
+    def copy(i, src, dst, target):
+        return pltpu.make_async_remote_copy(
+            src_ref=src,
+            dst_ref=dst,
+            send_sem=send.at[i],
+            recv_sem=recv.at[i],
+            device_id=target,
+            device_id_type=pl.DeviceIdType.MESH,
+        )
+
+    def head(r):
+        return (dp, block * 8 + (q + r) % 8)
+
+    def plane(r):
+        return (dp, ((block + r) % 16) * 8 + q)
+
+    peers = [head(r) for r in range(1, 8)] + [plane(r) for r in range(1, 16)]
+    peers += [(1 - dp, block * 8 + (q + r) % 8) for r in range(8)]
+    barrier = pltpu.get_barrier_semaphore()
+    for peer in peers:
+        pl.semaphore_signal(barrier, inc=1, device_id=peer, device_id_type=pl.DeviceIdType.MESH)
+    pl.semaphore_wait(barrier, len(peers))
+
+    own_rows = pl.ds(WINDOW, keys.shape[0])
+    last_rows = pl.ds(keys.shape[0] - WINDOW, WINDOW)
+    first_rows = pl.ds(0, WINDOW)
+
+    def page_rows(page):
+        return pl.ds(pl.multiple_of(page * PAGE_ROWS, PAGE_ROWS), PAGE_ROWS)
+
+    at = CONTEXT_COPIES
+    sent = []
+    for i, (source, target) in enumerate(((keys, key_window), (values, value_window))):
+        c = copy(at + i, source.at[last_rows], target.at[first_rows], plane(1))
+        c.start()
+        sent.append(c)
+    at += 2
+    for r in range(1, 16):
+        c = copy(at + r - 1, sink_pairs, sinks.at[block], plane(r))
+        c.start()
+        sent.append(c)
+    locals_now = [
+        pltpu.make_async_copy(keys, key_window.at[own_rows], local.at[0]),
+        pltpu.make_async_copy(values, value_window.at[own_rows], local.at[1]),
+        pltpu.make_async_copy(sink_pairs, sinks.at[block], local.at[2]),
+        pltpu.make_async_copy(keys.at[page_rows(q)], key_out.at[q], local.at[3]),
+        pltpu.make_async_copy(values.at[page_rows(q)], value_out.at[q], local.at[4]),
+    ]
+    for c in locals_now:
+        c.start()
+    at += 15
+    for r in range(1, 8):
+        page = (q + r) % 8
+        for i, (source, target) in enumerate(((keys, key_out), (values, value_out))):
+            c = copy(at + (r - 1) * 2 + i, source.at[page_rows(page)], target.at[q], head(r))
+            c.start()
+            sent.append(c)
+    at = CONTEXT_COPIES
+    for i, target in enumerate((key_window, value_window)):
+        copy(at + i, target.at[first_rows], target.at[first_rows], plane(1)).wait_recv()
+    at += 2
+    for r in range(1, 16):
+        landed = sinks.at[(block + 16 - r) % 16]
+        copy(at + r - 1, landed, landed, plane(1)).wait_recv()
+    for c in locals_now[:3]:
+        c.wait()
+
+    sink_sum = jnp.sum(sinks[...].astype(jnp.float32), 0).astype(jnp.bfloat16)
+    sink_keys, sink_values = sink_sum[0], sink_sum[1]
+    scale = HEAD_SIZE ** (-0.5)
+    last_dims = (((1,), (1,)), ((), ()))
+
+    def page_of(step):
+        return ((zh + 3 - step // 2) % 4) * 2 + (core + 1 + step) % 2
+
+    def columns(head_index):
+        return pl.ds(pl.multiple_of(head_index * width, width), width)
+
+    def to_half(step, half):
+        target = context.at[dp, :, columns(q)]
+        i = step if half == 0 else 8 + step
+        side = dp if half == 0 else 1 - dp
+        return copy(i, mixed.at[step], target, (side, block * 8 + page_of(step)))
+
+    def attend(step, carry):
+        page = page_of(step)
+        rows = page_rows(page)
+        row_start = starts[rows, :]
+        first = block * keys.shape[0] + page * PAGE_ROWS
+        query_pos = first + lax.broadcasted_iota(jnp.int32, (PAGE_ROWS, 1), 0)
+        key_pos = first - WINDOW + lax.broadcasted_iota(jnp.int32, (PAGE_ROWS, REACH), 1)
+        allowed = (
+            (key_pos <= query_pos) & (key_pos >= row_start) & (key_pos >= query_pos - WINDOW)
+        )
+        sink_pos = sink_rows[0:1, :]
+        sink_allowed = (
+            (sink_rows[1:2, :] == row_start)
+            & (sink_pos <= query_pos)
+            & (sink_pos < query_pos - WINDOW)
+        )
+        reach = pl.ds(pl.multiple_of(page * PAGE_ROWS, PAGE_ROWS), REACH)
+        near_keys = key_window[reach, :]
+        near_values = value_window[reach, :]
+        for h in range(width // HEAD_SIZE):
+            part = pl.ds(h * HEAD_SIZE, HEAD_SIZE)
+            query = queries[rows, part]
+            scores = (
+                lax.dot_general(query, near_keys, last_dims, preferred_element_type=jnp.float32)
+                * scale
+            )
+            sink_scores = (
+                lax.dot_general(query, sink_keys, last_dims, preferred_element_type=jnp.float32)
+                * scale
+            )
+            scores = jnp.where(allowed, scores, -jnp.inf)
+            sink_scores = jnp.where(sink_allowed, sink_scores, -jnp.inf)
+            top = jnp.maximum(
+                jnp.max(scores, -1, keepdims=True), jnp.max(sink_scores, -1, keepdims=True)
+            )
+            near = jnp.exp(scores - top)
+            far = jnp.exp(sink_scores - top)
+            inverse = 1.0 / (
+                jnp.sum(near, -1, keepdims=True) + jnp.sum(far, -1, keepdims=True)
+            )
+            result = jnp.dot(
+                (near * inverse).astype(jnp.bfloat16),
+                near_values,
+                preferred_element_type=jnp.float32,
+            ) + jnp.dot(
+                (far * inverse).astype(jnp.bfloat16),
+                sink_values,
+                preferred_element_type=jnp.float32,
+            )
+            mixed[step, :, part] = result.astype(jnp.bfloat16)
+
+        @pl.when(step > 0)
+        def _():
+            for half in range(2):
+                to_half(step - 1, half).start()
+
+        return carry
+
+    lax.fori_loop(0, 8, attend, 0)
+    at = CONTEXT_COPIES + 2 + 15
+    for r in range(1, 8):
+        for i, target in enumerate((key_out, value_out)):
+            landed = target.at[(q + 8 - r) % 8]
+            copy(at + (r - 1) * 2 + i, landed, landed, head(1)).wait_recv()
+    for c in sent:
+        c.wait_send()
+    for c in locals_now[3:]:
+        c.wait()
+    own = pltpu.make_async_copy(mixed.at[7], context.at[dp, :, columns(q)], local.at[5])
+    own.start()
+    to_half(7, 1).start()
+    for step in range(8):
+        source = ((zh + 4 - 3 + step // 2) % 4) * 2 + (core + 1 + step) % 2
+        for i, half in enumerate((dp, 1 - dp)):
+            if i == 0 and step == 7:
+                continue
+            landed = context.at[half, :, columns(source)]
+            copy(i * 8 + step, landed, landed, head(1)).wait_recv()
+    for step in range(8):
+        if step < 7:
+            to_half(step, 0).wait_send()
+        to_half(step, 1).wait_send()
+    own.wait()
+
+
+def attend_pages(queries, keys, values, starts, sink_rows, sink_pairs):
+    rows, width = queries.shape
+    vmem = pl.BlockSpec(memory_space=pltpu.VMEM)
+    hbm = pl.BlockSpec(memory_space=pltpu.HBM)
+    cache = jax.ShapeDtypeStruct((KEY_VALUE_HEADS, PAGE_ROWS, HEAD_SIZE), keys.dtype)
+    return pl.pallas_call(
+        attend_kernel,
+        out_shape=(
+            jax.ShapeDtypeStruct((2, PAGE_ROWS, KEY_VALUE_HEADS * width), queries.dtype),
+            cache,
+            cache,
+        ),
+        in_specs=[vmem] * 6,
+        out_specs=(hbm,) * 3,
+        scratch_shapes=[
+            pltpu.VMEM((WINDOW + rows, HEAD_SIZE), keys.dtype),
+            pltpu.VMEM((WINDOW + rows, HEAD_SIZE), keys.dtype),
+            pltpu.VMEM((16,) + sink_pairs.shape, sink_pairs.dtype),
+            pltpu.VMEM((8, PAGE_ROWS, width), queries.dtype),
+            pltpu.SemaphoreType.DMA((ATTEND_COPIES,)),
+            pltpu.SemaphoreType.DMA((ATTEND_COPIES,)),
+            pltpu.SemaphoreType.DMA((6,)),
+        ],
+        compiler_params=pltpu.CompilerParams(collective_id=1, has_side_effects=True),
+        name="attend",
+    )(queries, keys, values, starts, sink_rows, sink_pairs)
+
+
 def body(tokens, norm_gain, segments, deal_table, projection):
     group_id = lax.axis_index("dp")
     device_number = lax.axis_index("tensor")
-    tensor_width = lax.axis_size("tensor")
     token_per_device = tokens.shape[1]
     model_width = tokens.shape[2]
     block_length = KEY_VALUE_HEADS * token_per_device
     block_number = device_number // KEY_VALUE_HEADS
     group_queries = QUERY_HEADS // KEY_VALUE_HEADS
-    head_bit_flags = KEY_VALUE_HEADS.bit_length() - 1
-    level_bits = tensor_width.bit_length() - 1
     own_page = tokens[0]
     owner_group = jnp.sum(jnp.where(jnp.arange(deal_table.shape[1]) == group_id, deal_table[0], 0))
     stay_here = owner_group == group_id
@@ -282,119 +488,24 @@
         projected[:, group_queries * HEAD_SIZE : (group_queries + 1) * HEAD_SIZE], angles
     ).astype(jnp.bfloat16)
     values_own = projected[:, (group_queries + 1) * HEAD_SIZE :].astype(jnp.bfloat16)
-    local_pairs = jnp.concatenate((keys_own, values_own), 1)
-    reach_blocks = -(-WINDOW // block_length)
-    previous_pairs = [shifted(local_pairs, "tensor", 1 * KEY_VALUE_HEADS)]
-    window_pairs = jnp.concatenate(previous_pairs + [local_pairs], 0)
+    local_pairs = jnp.stack((keys_own, values_own))
     sink_positions = (seg_starts[:, None] + jnp.arange(SINKS)[None, :]).reshape(NSEG * SINKS)
     local_rows = sink_positions - block_number * block_length
     selector = (local_rows[:, None] == jnp.arange(block_length)[None, :]).astype(jnp.bfloat16)
-    sink_flat = jnp.dot(selector, local_pairs, preferred_element_type=jnp.float32).astype(
-        jnp.bfloat16
+    sink_pairs = jnp.einsum(
+        "sr,prd->psd", selector, local_pairs, preferred_element_type=jnp.float32
+    ).astype(jnp.bfloat16)
+    sink_rows = jnp.stack((sink_positions, jnp.repeat(seg_starts, SINKS)))
+    contexts, key_cache, value_cache = attend_pages(
+        queries.reshape(block_length, group_queries * HEAD_SIZE),
+        keys_own,
+        values_own,
+        starts_block[:, None],
+        sink_rows,
+        sink_pairs,
     )
-    for bit_index in range(head_bit_flags, level_bits):
-        sink_flat = sink_flat + from_partner(sink_flat, "tensor", bit_index)
-    sink_pairs = sink_flat.reshape(NSEG, SINKS, 2 * HEAD_SIZE)
-    tile_rows = min(512, block_length)
-    score_scale = HEAD_SIZE ** (-0.5)
-
-    def attend(tile_start):
-        query_tile = lax.dynamic_slice_in_dim(queries, tile_start, tile_rows, 0)
-        query_pos = block_number * block_length + tile_start + jnp.arange(tile_rows)
-        query_start = lax.dynamic_slice_in_dim(starts_block, tile_start, tile_rows, 0)
-        key_from = reach_blocks * block_length + tile_start - WINDOW
-        key_pairs = lax.dynamic_slice_in_dim(window_pairs, key_from, WINDOW + tile_rows, 0)
-        key_pos = (
-            (block_number - reach_blocks) * block_length + key_from + jnp.arange(WINDOW + tile_rows)
-        )
-        scores = (
-            jnp.einsum(
-                "rgd,kd->rgk",
-                query_tile,
-                key_pairs[:, :HEAD_SIZE],
-                preferred_element_type=jnp.float32,
-            )
-            * score_scale
-        )
-        allowed = (
-            (key_pos[None, :] <= query_pos[:, None])
-            & (key_pos[None, :] >= query_start[:, None])
-            & (key_pos[None, :] >= query_pos[:, None] - WINDOW)
-        )
-        chooser = (seg_starts[None, :] == query_start[:, None]).astype(jnp.bfloat16)
-        row_sinks = jnp.einsum(
-            "rs,sqc->rqc", chooser, sink_pairs, preferred_element_type=jnp.float32
-        ).astype(jnp.bfloat16)
-        sink_scores = (
-            jnp.einsum(
-                "rgd,rqd->rgq",
-                query_tile,
-                row_sinks[:, :, :HEAD_SIZE],
-                preferred_element_type=jnp.float32,
-            )
-            * score_scale
-        )
-        sink_pos = query_start[:, None] + jnp.arange(SINKS)[None, :]
-        sink_allowed = (sink_pos <= query_pos[:, None]) & (sink_pos < query_pos[:, None] - WINDOW)
-        masked = jnp.where(allowed[:, None, :], scores, -jnp.inf)
-        masked_sinks = jnp.where(sink_allowed[:, None, :], sink_scores, -jnp.inf)
-        top_score = jnp.maximum(
-            jnp.max(masked, -1, keepdims=True), jnp.max(masked_sinks, -1, keepdims=True)
-        )
-        window_weights = jnp.exp(masked - top_score)
-        sink_weights = jnp.exp(masked_sinks - top_score)
-        denominator = jnp.sum(window_weights, -1, keepdims=True) + jnp.sum(
-            sink_weights, -1, keepdims=True
-        )
-        window_probs = (window_weights / denominator).astype(jnp.bfloat16)
-        sink_probs = (sink_weights / denominator).astype(jnp.bfloat16)
-        mixed_rows = jnp.einsum(
-            "rgk,kd->rgd",
-            window_probs,
-            key_pairs[:, HEAD_SIZE:],
-            preferred_element_type=jnp.float32,
-        )
-        mixed_rows = mixed_rows + jnp.einsum(
-            "rgq,rqd->rgd",
-            sink_probs,
-            row_sinks[:, :, HEAD_SIZE:],
-            preferred_element_type=jnp.float32,
-        )
-        return mixed_rows.astype(jnp.bfloat16).reshape(tile_rows, group_queries * HEAD_SIZE)
-
-    tile_offsets = jnp.arange(block_length // tile_rows, dtype=jnp.int32) * tile_rows
-    context_block = lax.map(attend, tile_offsets).reshape(block_length, group_queries * HEAD_SIZE)
-    pairs_by_dest = local_pairs.reshape((2,) * head_bit_flags + (token_per_device, 2 * HEAD_SIZE))
-    context_by_dest = context_block.reshape(
-        (2,) * head_bit_flags + (token_per_device, group_queries * HEAD_SIZE)
-    )
-    kept_pairs = pairs_by_dest
-    for bit_index in range(head_bit_flags):
-        axis_pos = head_bit_flags - 1 - bit_index
-        bit_value = device_number >> bit_index & 1
-        own_half = lax.dynamic_index_in_dim(kept_pairs, bit_value, axis_pos, keepdims=False)
-        sent_half = lax.dynamic_index_in_dim(kept_pairs, 1 - bit_value, axis_pos, keepdims=False)
-        arrived = from_partner(sent_half, "tensor", bit_index)
-        kept_pairs = stack_pair(own_half, arrived, bit_value == 1, axis_pos)
-    kept_context = context_by_dest
-    for bit_index in range(head_bit_flags):
-        axis_pos = head_bit_flags - 1 - bit_index
-        bit_value = device_number >> bit_index & 1
-        own_half = lax.dynamic_index_in_dim(kept_context, bit_value, axis_pos, keepdims=False)
-        sent_half = lax.dynamic_index_in_dim(kept_context, 1 - bit_value, axis_pos, keepdims=False)
-        arrived = from_partner(sent_half, "tensor", bit_index)
-        kept_context = stack_pair(own_half, arrived, bit_value == 1, axis_pos)
-    cached_heads = kept_pairs.reshape(KEY_VALUE_HEADS, token_per_device, 2 * HEAD_SIZE)
-    key_cache = cached_heads[:, :, :HEAD_SIZE][None]
-    value_cache = cached_heads[:, :, HEAD_SIZE:][None]
-    context_local = (
-        kept_context.reshape(KEY_VALUE_HEADS, token_per_device, group_queries * HEAD_SIZE)
-        .transpose(1, 0, 2)
-        .reshape(token_per_device, QUERY_HEADS * HEAD_SIZE)
-    )
-    context_back = from_partner(context_local, "dp", 0)
-    context = jnp.where(stay_here, context_local, context_back)[None]
-    return (context, key_cache, value_cache)
+    context = jnp.where(owner_group == 1, contexts[1], contexts[0])
+    return (context[None], key_cache[None], value_cache[None])
 
 
 def solution(mesh):

time: 319 us -> 222 us (0.70)
  Pallas kernels: 93.7 us -> 170 us
  waiting for transfers between devices: 72.2 us -> 0 us
  starting transfers between devices: 37.6 us -> 0 us
  matrix products: 34.9 us -> 9.96 us
  local copies, waits for them, and re-layouts: 30.5 us -> 13.3 us
  other arithmetic: 38.1 us -> 23.9 us
  loops' own time: 8.08 us -> 0 us
    pallas_call x0 -> x1, Pallas kernels: none -> 76.5 us  [attend_pages(): pl.pallas_call(attend_kernel, out_shape=(jax.ShapeDtypeStruct((2, PAGE_RO...]
    ppermute x12 -> x0, waiting for transfers between devices: 72.2 us -> none  [the longest x11 72.2 us: from_partner(): return lax.ppermute(value, axis, pairs)]
    ppermute x12 -> x0, starting transfers between devices: 37.6 us -> none  [the longest x11 33.4 us: from_partner(): return lax.ppermute(value, axis, pairs)]
    dot_general x11 -> x1, matrix products: 25.8 us -> 0.87 us  [body(): jnp.einsum('sr,prd->psd', selector, local_pairs, preferred_element_type=j...]
    reduce_sum x4 -> x0, other arithmetic: 9.41 us -> none  [the longest x2 9.32 us: attend(): jnp.sum(window_weights, -1, keepdims=True)]
    another operation x1 -> x0, loops' own time: 8.08 us -> none  [body(): lax.map(attend, tile_offsets)]
    dynamic_slice x7 -> x0, local copies, waits for them, and re-layouts: 5.81 us -> none  [the longest x2 2.43 us: body(): lax.map(attend, tile_offsets)]
    another operation x13 -> x4, other arithmetic: 7.14 us -> 6.44 us  [the longest x10 3.59 us: stack_pair(): return jnp.stack((lower_part, upper_part), axis=axis_pos)]
  transfers between devices with their start and end apart: 12 -> 0, of which waited for: 9 -> 0; matrix products, arithmetic and copies ran while one was open for 7% -> 0% of each run, Pallas kernels for 0% -> 0%
where the time goes in v3:
time: 222 us; the launch traced here: 220 us
  Pallas kernels  170 us (77%)
  other arithmetic  23.9 us (11%)
  local copies, waits for them, and re-layouts  13.3 us (6%)
  matrix products  9.96 us (4%)
    pallas_call x1, Pallas kernels, gather(): pl.pallas_call(gather_kernel, out_shape=(jax.ShapeDtypeStruct((8, 2, 2, r...  93.7 us
    pallas_call x1, Pallas kernels, attend_pages(): pl.pallas_call(attend_kernel, out_shape=(jax.ShapeDtypeStruct((2, PAGE_RO...  76.5 us
    dot_general x1, matrix products, body(): jnp.dot(rows_block, weights_held, preferred_element_type=jnp.float32)  9.08 us
    unnamed x16, local copies, waits for them, and re-layouts  7.47 us
    select_n x1, other arithmetic, body(): jnp.where(clients == 1, pages[:, 1], pages[:, 0])  6.62 us
    another operation x3, other arithmetic  5.83 us

profile of v3, /device:TPU:32, one launch (start us, length us, event | category | flops | bytes accessed | tf_op | source)
XLA Modules:
  0.0 219.5 jit_solution(11055578664322174230)
XLA Ops:
  0.7 1.3 fusion.10
  3.2 1.2 concatenate.25
  4.5 1.5 multiply_reduce_fusion
  6.2 2.5 %multiply_convert_fusion.page = bf16[2,64,4096]{2,1,0:T(8,128)(2,1)} fusion(f32[4096]{0:T(1024)} %param.6, f32[2,64]{1,0:T(2,128)S(1)} %rsqrt.12, bf16[2,64,4096]{2,1,0:T(8,128)(2,1)} %bitcast.45), kind=kLoop, calls=%fused_computation.3 | loop fusion | flops 2097152 | bytes 2114048 | tf_op jit(solution)/shard_map/convert_element_type | solution.py:460
  8.7 93.7 %gather.1 = (bf16[8,2,2,64,4096]{4,3,2,1,0:T(8,128)(2,1)}, bf16[16,2,2,64,768]{4,3,2,1,0:T(8,128)(2,1)}, s32[4,4,8,1,256]{4,3,2,1,0:T(1,128)}) custom-call(bf16[2,64,4096]{2,1,0:T(8,128)(2,1)} %multiply_convert_fusion.page, bf16[2,2,64,768]{3,2,1,0:T(8,128)(2,1)} %bitcast.50, s32[1,256]{1,0:T(1,128)} %bitcast.57), custom_call_target="tpu_custom_call" | custom-call | tf_op jit(solution)/shard_map/gather/pallas_call | solution.py:196
  102.4 0.9 copy.28
  104.1 6.6 %slice_select_fusion = bf16[4,1,2,128,4096]{4,3,2,1,0:T(8,128)(2,1)S(1)} fusion(bf16[4,2,2,128,4096]{4,3,2,1,0:T(8,128)(2,1)} %bitcast.41, pred[4,2]{1,0:T(4,128)(4,1)S(1)} %eq.71), kind=kLoop, calls=%fused_computation | loop fusion | flops 4194304 | bytes 25165832 | tf_op jit(solution)/shard_map/jit(_where)/select_n | solution.py:476
  110.7 9.1 %fusion.14 = f32[1024,768]{0,1:T(8,128)S(1)} fusion(bf16[1024,4096]{1,0:T(8,128)(2,1)S(1)} %bitcast.42, bf16[4096,768]{1,0:T(8,128)(2,1)} %bitcast.60), kind=kOutput, calls=%fused_computation.43 | convolution fusion | flops 6442450944 | bytes 17825792 | tf_op jit(solution)/shard_map/dot_general | solution.py:479
  120.8 0.8 copy.39.values
  121.7 1.0 copy.34.starts
  122.7 0.7 fusion.12
  123.7 1.2 fusion.13
  125.3 3.2 %subtract_convert_fusion.1 = (bf16[1024,64]{1,0:T(8,128)(2,1)S(1)}, bf16[1024,64]{1,0:T(8,128)(2,1)S(1)}, f32[1024,64]{1,0:T(8,128)}, f32[1024,64]{1,0:T(8,128)}) fusion(f32[1024,64]{1,0:T(8,128)S(1)} %copy.38, f32[1024,64]{1,0:T(8,128)S(1)} %copy.37, f32[64]{0:T(128)S(1)} %negate_power_fusion, f32[1024]{0:T(1024)S(1)} %subtract_convert_fusion.2), kind=kLoop, calls=%fused_computation.18 | loop fusion | flops 589824 | bytes 1315072 | tf_op jit(solution)/shard_map/convert.6
  128.4 0.9 fusion.sink_pairs
  129.3 0.8 pad_maximum_fusion.1.keys
  130.2 1.8 copy.36
  132.0 1.8 copy.35
  133.8 2.5 %subtract_convert_fusion = (bf16[1024,4,64]{2,1,0:T(4,128)(2,1)S(1)}, bf16[1024,4,64]{2,1,0:T(4,128)(2,1)S(1)}) fusion(f32[1024,4,64]{2,1,0:T(4,128)S(1)} %copy.36, f32[1024,4,64]{2,1,0:T(4,128)} %copy.35, f32[1024,64]{1,0:T(8,128)} %get-tuple-element.23, f32[1024,64]{1,0:T(8,128)} %get-tuple-element.24), kind=kLoop, calls=%fused_computation.2 | loop fusion | flops 2097152 | bytes 3670016 | tf_op jit(solution)/shard_map/convert.8
  136.3 1.4 pad_maximum_fusion
  137.7 1.2 copy.42
  138.9 76.5 %attend.1 = (bf16[2,128,4096]{2,1,0:T(8,128)(2,1)}, bf16[8,128,128]{2,1,0:T(8,128)(2,1)}, bf16[8,128,128]{2,1,0:T(8,128)(2,1)}) custom-call(bf16[1024,512]{1,0:T(8,128)(2,1)} %bitcast.46, bf16[1024,128]{1,0:T(8,128)(2,1)} %pad_maximum_fusion.1.keys, bf16[1024,128]{1,0:T(8,128)(2,1)} %copy.39.values, s32[1024,1]{1,0:T(8,128)} %copy.34.starts, ...), custom_call_target="tpu_custom_call" | custom-call | tf_op jit(solution)/shard_map/attend/pallas_call | solution.py:423
  215.4 2.7 %slice_select_fusion.1 = bf16[1,128,4096]{2,1,0:T(8,128)(2,1)} fusion(bf16[2,128,4096]{2,1,0:T(8,128)(2,1)} %get-tuple-element.12, pred[]{:T(512)S(6)} %eq.68), kind=kLoop, calls=%fused_computation.9 | loop fusion | flops 524288 | bytes 3145729 | tf_op jit(solution)/shard_map/jit(_where)/select_n | solution.py:507
  218.1 0.7 copy.45
  218.8 0.7 copy.46
  (33 shorter events, 2.5 us)
Async XLA Ops:
  123.7 1.2 copy-start
  124.9 3.6 %copy-start.1 = (bf16[1024,128]{1,0:T(8,128)(2,1)S(1)}, bf16[1024,128]{1,0:T(8,128)(2,1)}, u32[]{:S(2)}) copy-start(bf16[1024,128]{1,0:T(8,128)(2,1)} %copy.39.values) | copy-start | bytes 786436
  215.4 2.7 %copy-start.3 = (bf16[8,128,128]{2,1,0:T(8,128)(2,1)S(1)}, bf16[8,128,128]{2,1,0:T(8,128)(2,1)}, u32[]{:S(2)}) copy-start(bf16[8,128,128]{2,1,0:T(8,128)(2,1)} %get-tuple-element.13) | copy-start | bytes 786436
  215.4 3.4 %copy-start.2 = (bf16[8,128,128]{2,1,0:T(8,128)(2,1)S(1)}, bf16[8,128,128]{2,1,0:T(8,128)(2,1)}, u32[]{:S(2)}) copy-start(bf16[8,128,128]{2,1,0:T(8,128)(2,1)} %get-tuple-element.14) | copy-start | bytes 786436

commit v4 on v3

--- a/solution.py
+++ b/solution.py
@@ -219,7 +219,8 @@
 PAGE_ROWS = 128
 REACH = WINDOW + PAGE_ROWS
 CONTEXT_COPIES = 16
-ATTEND_COPIES = CONTEXT_COPIES + 14 + 2 + 15
+ATTEND_COPIES = CONTEXT_COPIES + 2 + 15 + 16 + 4
+FAR = 2
 
 
 def attend_kernel(
@@ -236,6 +237,7 @@
     value_window,
     sinks,
     mixed,
+    passing,
     send,
     recv,
     local,
@@ -258,6 +260,11 @@
 
     def head(r):
         return (dp, block * 8 + (q + r) % 8)
+
+    def page_near(shift, flip):
+        return ((zh + shift) % 4) * 2 + (core + flip) % 2
+
+    partner = (1 - dp, t)
 
     def plane(r):
         return (dp, ((block + r) % 16) * 8 + q)
@@ -296,13 +303,33 @@
     ]
     for c in locals_now:
         c.start()
-    at += 15
-    for r in range(1, 8):
-        page = (q + r) % 8
-        for i, (source, target) in enumerate(((keys, key_out), (values, value_out))):
-            c = copy(at + (r - 1) * 2 + i, source.at[page_rows(page)], target.at[q], head(r))
+    caches = ((keys, key_out), (values, value_out))
+    spread = [(shift, flip) for shift in (FAR, 3, 1, 0) for flip in (1, 0)][:7]
+
+    def cache_slot(shift, flip, i):
+        return CONTEXT_COPIES + 17 + (shift * 2 + flip) * 2 + i
+
+    def passing_slot(flip, i):
+        return CONTEXT_COPIES + 33 + flip * 2 + i
+
+    for shift, flip in spread:
+        page = page_near(shift, flip)
+        for i, (source, target) in enumerate(caches):
+            piece = source.at[page_rows(page)]
+            if shift == FAR:
+                c = copy(
+                    passing_slot(flip, i), piece, passing.at[i, flip], (1 - dp, block * 8 + page)
+                )
+            else:
+                c = copy(cache_slot(shift, flip, i), piece, target.at[q], (dp, block * 8 + page))
             c.start()
             sent.append(c)
+
+    def hand_on(flip, i):
+        piece = passing.at[i, flip]
+        source = page_near(4 - FAR, flip)
+        return copy(cache_slot(FAR, flip, i), piece, caches[i][1].at[source], partner)
+
     at = CONTEXT_COPIES
     for i, target in enumerate((key_window, value_window)):
         copy(at + i, target.at[first_rows], target.at[first_rows], plane(1)).wait_recv()
@@ -319,7 +346,8 @@
     last_dims = (((1,), (1,)), ((), ()))
 
     def page_of(step):
-        return ((zh + 3 - step // 2) % 4) * 2 + (core + 1 + step) % 2
+        turn = step // 2
+        return page_near(FAR + turn * (turn + 1) // 2, 1 + step)
 
     def columns(head_index):
         return pl.ds(pl.multiple_of(head_index * width, width), width)
@@ -383,33 +411,58 @@
 
         @pl.when(step > 0)
         def _():
-            for half in range(2):
-                to_half(step - 1, half).start()
+            to_half(step - 1, 1).start()
+
+        @pl.when(step > 2)
+        def _():
+            to_half(step - 1, 0).start()
+
+        @pl.when(step == 2)
+        def _():
+            for flip in range(2):
+                for i in range(2):
+                    piece = passing.at[i, flip]
+                    copy(passing_slot(flip, i), piece, piece, partner).wait_recv()
+                    hand_on(flip, i).start()
 
         return carry
 
     lax.fori_loop(0, 8, attend, 0)
-    at = CONTEXT_COPIES + 2 + 15
-    for r in range(1, 8):
-        for i, target in enumerate((key_out, value_out)):
-            landed = target.at[(q + 8 - r) % 8]
-            copy(at + (r - 1) * 2 + i, landed, landed, head(1)).wait_recv()
-    for c in sent:
+    own = pltpu.make_async_copy(mixed.at[7], context.at[dp, :, columns(q)], local.at[5])
+    own.start()
+    to_half(7, 1).start()
+
+    def source_of(step):
+        turn = step // 2
+        return page_near(8 - FAR - turn * (turn + 1) // 2, 1 + step)
+
+    def landed(step, half):
+        return context.at[dp if half == 0 else 1 - dp, :, columns(source_of(step))]
+
+    def pass_context(step):
+        piece = landed(step, 1)
+        return copy(step, piece, piece, partner)
+
+    for step in range(2):
+        copy(8 + step, landed(step, 1), landed(step, 1), partner).wait_recv()
+        pass_context(step).start()
+    for shift, flip in spread:
+        source = page_near(4 - shift, flip)
+        for i in range(2):
+            piece = caches[i][1].at[source]
+            copy(cache_slot(shift, flip, i), piece, piece, partner).wait_recv()
+    for step in range(2, 8):
+        copy(8 + step, landed(step, 1), landed(step, 1), partner).wait_recv()
+    for step in range(7):
+        copy(step, landed(step, 0), landed(step, 0), partner).wait_recv()
+    for c in sent + [hand_on(flip, i) for flip in range(2) for i in range(2)]:
         c.wait_send()
     for c in locals_now[3:]:
         c.wait()
-    own = pltpu.make_async_copy(mixed.at[7], context.at[dp, :, columns(q)], local.at[5])
-    own.start()
-    to_half(7, 1).start()
     for step in range(8):
-        source = ((zh + 4 - 3 + step // 2) % 4) * 2 + (core + 1 + step) % 2
-        for i, half in enumerate((dp, 1 - dp)):
-            if i == 0 and step == 7:
-                continue
-            landed = context.at[half, :, columns(source)]
-            copy(i * 8 + step, landed, landed, head(1)).wait_recv()
-    for step in range(8):
-        if step < 7:
+        if step < 2:
+            pass_context(step).wait_send()
+        elif step < 7:
             to_half(step, 0).wait_send()
         to_half(step, 1).wait_send()
     own.wait()
@@ -434,6 +487,7 @@
             pltpu.VMEM((WINDOW + rows, HEAD_SIZE), keys.dtype),
             pltpu.VMEM((16,) + sink_pairs.shape, sink_pairs.dtype),
             pltpu.VMEM((8, PAGE_ROWS, width), queries.dtype),
+            pltpu.VMEM((2, 2, PAGE_ROWS, HEAD_SIZE), keys.dtype),
             pltpu.SemaphoreType.DMA((ATTEND_COPIES,)),
             pltpu.SemaphoreType.DMA((ATTEND_COPIES,)),
             pltpu.SemaphoreType.DMA((6,)),

time: 222 us -> 216 us (0.973)
  Pallas kernels: 170 us -> 166 us
    pallas_call x1, Pallas kernels: 76.5 us -> 72.7 us  [attend_pages(): pl.pallas_call(attend_kernel, out_shape=(jax.ShapeDtypeStruct((2, PAGE_RO...]
where the time goes in v4:
time: 216 us
  Pallas kernels  166 us (77%)
  other arithmetic  23.9 us (11%)
  local copies, waits for them, and re-layouts  13.3 us (6%)
  matrix products  9.96 us (5%)
    pallas_call x1, Pallas kernels, gather(): pl.pallas_call(gather_kernel, out_shape=(jax.ShapeDtypeStruct((8, 2, 2, r...  93.7 us
    pallas_call x1, Pallas kernels, attend_pages(): pl.pallas_call(attend_kernel, out_shape=(jax.ShapeDtypeStruct((2, PAGE_RO...  72.7 us
    dot_general x1, matrix products, body(): jnp.dot(rows_block, weights_held, preferred_element_type=jnp.float32)  9.08 us
    unnamed x16, local copies, waits for them, and re-layouts  7.47 us
    select_n x1, other arithmetic, body(): jnp.where(clients == 1, pages[:, 1], pages[:, 0])  6.62 us
    another operation x3, other arithmetic  5.83 us

profile of v4, /device:TPU:32, one launch (start us, length us, event | category | flops | bytes accessed | tf_op | source)
XLA Modules:
  0.0 215.7 jit_solution(1222704182485734394)
XLA Ops:
  0.7 1.3 fusion.10
  3.2 1.2 concatenate.25
  4.5 1.5 multiply_reduce_fusion
  6.2 2.5 %multiply_convert_fusion.page = bf16[2,64,4096]{2,1,0:T(8,128)(2,1)} fusion(f32[4096]{0:T(1024)} %param.6, f32[2,64]{1,0:T(2,128)S(1)} %rsqrt.12, bf16[2,64,4096]{2,1,0:T(8,128)(2,1)} %bitcast.45), kind=kLoop, calls=%fused_computation.3 | loop fusion | flops 2097152 | bytes 2114048 | tf_op jit(solution)/shard_map/convert_element_type | solution.py:514
  8.7 93.7 %gather.1 = (bf16[8,2,2,64,4096]{4,3,2,1,0:T(8,128)(2,1)}, bf16[16,2,2,64,768]{4,3,2,1,0:T(8,128)(2,1)}, s32[4,4,8,1,256]{4,3,2,1,0:T(1,128)}) custom-call(bf16[2,64,4096]{2,1,0:T(8,128)(2,1)} %multiply_convert_fusion.page, bf16[2,2,64,768]{3,2,1,0:T(8,128)(2,1)} %bitcast.50, s32[1,256]{1,0:T(1,128)} %bitcast.57), custom_call_target="tpu_custom_call" | custom-call | tf_op jit(solution)/shard_map/gather/pallas_call | solution.py:196
  102.4 0.9 copy.28
  104.1 6.6 %slice_select_fusion = bf16[4,1,2,128,4096]{4,3,2,1,0:T(8,128)(2,1)S(1)} fusion(bf16[4,2,2,128,4096]{4,3,2,1,0:T(8,128)(2,1)} %bitcast.41, pred[4,2]{1,0:T(4,128)(4,1)S(1)} %eq.71), kind=kLoop, calls=%fused_computation | loop fusion | flops 4194304 | bytes 25165832 | tf_op jit(solution)/shard_map/jit(_where)/select_n | solution.py:530
  110.7 9.1 %fusion.14 = f32[1024,768]{0,1:T(8,128)S(1)} fusion(bf16[1024,4096]{1,0:T(8,128)(2,1)S(1)} %bitcast.42, bf16[4096,768]{1,0:T(8,128)(2,1)} %bitcast.60), kind=kOutput, calls=%fused_computation.43 | convolution fusion | flops 6442450944 | bytes 17825792 | tf_op jit(solution)/shard_map/dot_general | solution.py:533
  120.8 0.8 copy.39.values
  121.7 1.0 copy.34.starts
  122.7 0.7 fusion.12
  123.7 1.2 fusion.13
  125.3 3.2 %subtract_convert_fusion.1 = (bf16[1024,64]{1,0:T(8,128)(2,1)S(1)}, bf16[1024,64]{1,0:T(8,128)(2,1)S(1)}, f32[1024,64]{1,0:T(8,128)}, f32[1024,64]{1,0:T(8,128)}) fusion(f32[1024,64]{1,0:T(8,128)S(1)} %copy.38, f32[1024,64]{1,0:T(8,128)S(1)} %copy.37, f32[64]{0:T(128)S(1)} %negate_power_fusion, f32[1024]{0:T(1024)S(1)} %subtract_convert_fusion.2), kind=kLoop, calls=%fused_computation.18 | loop fusion | flops 589824 | bytes 1315072 | tf_op jit(solution)/shard_map/convert.6
  128.4 0.9 fusion.sink_pairs
  129.3 0.8 pad_maximum_fusion.1.keys
  130.2 1.8 copy.36
  132.0 1.8 copy.35
  133.8 2.5 %subtract_convert_fusion = (bf16[1024,4,64]{2,1,0:T(4,128)(2,1)S(1)}, bf16[1024,4,64]{2,1,0:T(4,128)(2,1)S(1)}) fusion(f32[1024,4,64]{2,1,0:T(4,128)S(1)} %copy.36, f32[1024,4,64]{2,1,0:T(4,128)} %copy.35, f32[1024,64]{1,0:T(8,128)} %get-tuple-element.23, f32[1024,64]{1,0:T(8,128)} %get-tuple-element.24), kind=kLoop, calls=%fused_computation.2 | loop fusion | flops 2097152 | bytes 3670016 | tf_op jit(solution)/shard_map/convert.8
  136.3 1.4 pad_maximum_fusion
  137.7 1.2 copy.42
  138.9 72.7 %attend.1 = (bf16[2,128,4096]{2,1,0:T(8,128)(2,1)}, bf16[8,128,128]{2,1,0:T(8,128)(2,1)}, bf16[8,128,128]{2,1,0:T(8,128)(2,1)}) custom-call(bf16[1024,512]{1,0:T(8,128)(2,1)} %bitcast.46, bf16[1024,128]{1,0:T(8,128)(2,1)} %pad_maximum_fusion.1.keys, bf16[1024,128]{1,0:T(8,128)(2,1)} %copy.39.values, s32[1024,1]{1,0:T(8,128)} %copy.34.starts, ...), custom_call_target="tpu_custom_call" | custom-call | tf_op jit(solution)/shard_map/attend/pallas_call | solution.py:476
  211.6 2.7 %slice_select_fusion.1 = bf16[1,128,4096]{2,1,0:T(8,128)(2,1)} fusion(bf16[2,128,4096]{2,1,0:T(8,128)(2,1)} %get-tuple-element.12, pred[]{:T(512)S(6)} %eq.68), kind=kLoop, calls=%fused_computation.9 | loop fusion | flops 524288 | bytes 3145729 | tf_op jit(solution)/shard_map/jit(_where)/select_n | solution.py:561
  214.3 0.7 copy.45
  215.0 0.7 copy.46
  (33 shorter events, 2.5 us)
Async XLA Ops:
  123.7 1.2 copy-start
  124.9 3.6 %copy-start.1 = (bf16[1024,128]{1,0:T(8,128)(2,1)S(1)}, bf16[1024,128]{1,0:T(8,128)(2,1)}, u32[]{:S(2)}) copy-start(bf16[1024,128]{1,0:T(8,128)(2,1)} %copy.39.values) | copy-start | bytes 786436
  211.6 2.7 %copy-start.3 = (bf16[8,128,128]{2,1,0:T(8,128)(2,1)S(1)}, bf16[8,128,128]{2,1,0:T(8,128)(2,1)}, u32[]{:S(2)}) copy-start(bf16[8,128,128]{2,1,0:T(8,128)(2,1)} %get-tuple-element.13) | copy-start | bytes 786436
  211.6 3.4 %copy-start.2 = (bf16[8,128,128]{2,1,0:T(8,128)(2,1)S(1)}, bf16[8,128,128]{2,1,0:T(8,128)(2,1)}, u32[]{:S(2)}) copy-start(bf16[8,128,128]{2,1,0:T(8,128)(2,1)} %get-tuple-element.14) | copy-start | bytes 786436

commit v5 on v4

--- a/solution.py
+++ b/solution.py
@@ -17,22 +17,26 @@
 norm_eps = 1e-05
 
 
-def rotary(values, angles):
-    half_width = values.shape[-1] // 2
-    first_half = values[..., :half_width]
-    second_half = values[..., half_width:]
-    cosine = jnp.cos(angles)
-    sine_part = jnp.sin(angles)
-    return jnp.concatenate(
-        (
-            first_half * cosine - second_half * sine_part,
-            second_half * cosine + first_half * sine_part,
-        ),
-        -1,
-    )
-
-
-def gather_kernel(page, slab, note, pages, weights, notes, send, recv, local):
+def gather_kernel(
+    page,
+    slab,
+    note,
+    gain,
+    freq,
+    queries,
+    keys,
+    values,
+    starts,
+    sink_rows,
+    sink_pairs,
+    pages,
+    weights,
+    notes,
+    normed,
+    send,
+    recv,
+    local,
+):
     dp = lax.axis_index("dp")
     t = lax.axis_index("tensor")
     core, zh = t % 2, (t // 2) % 4
@@ -91,6 +95,116 @@
         dx, dy = (da, db) if order == 0 else (db, da)
         return device(dx + 4, dy + 4, z, core)
 
+    page_count = 2 * page.shape[1]
+    pair_count = 2 * page_count
+    model_width = page.shape[2]
+    query_width = queries.shape[1]
+    depth = 4 * slab.shape[2]
+    per_step = model_width // 4
+    block = x * 4 + y
+
+    def seg_starts():
+        ids = notes[:, :, :, :, 0:page_count]
+        found = []
+        for segment in range(NSEG):
+            below = jnp.sum((ids < segment).astype(jnp.float32), (0, 1, 2))
+            found.append(jnp.sum(below, -1, keepdims=True))
+        return found
+
+    def rotated(block_values, cosine, sine):
+        half = HEAD_SIZE // 2
+        first, second = block_values[:, :half], block_values[:, half:]
+        return jnp.concatenate(
+            (first * cosine - second * sine, second * cosine + first * sine), -1
+        ).astype(jnp.bfloat16)
+
+    def project(shift):
+        pair = (zh + shift) % 4
+        found = seg_starts()
+        eye = lax.broadcasted_iota(jnp.int32, (page_count, page_count), 0)
+        eye = eye == lax.broadcasted_iota(jnp.int32, (page_count, page_count), 1)
+        columns = []
+        for c in range(2):
+            told = notes[y, x, pair * 2 + c]
+            ids, client = told[:, :page_count], told[:, page_count:]
+            start_row = jnp.zeros(ids.shape, jnp.float32)
+            for segment in range(NSEG):
+                start_row = jnp.where(ids == segment, found[segment], start_row)
+            start_row = jnp.broadcast_to(start_row, (page_count, page_count))
+            columns.append(jnp.sum(jnp.where(eye, start_row, 0.0), 1, keepdims=True))
+            upper = jnp.tile(client, (1, model_width // page_count)) == 1
+            upper = jnp.broadcast_to(upper, (16, model_width))
+            for h in range(2):
+
+                def norm(i, carry, c=c, h=h, upper=upper):
+                    rows = pl.ds(pl.multiple_of(i * 16, 16), 16)
+                    wide = jnp.where(
+                        upper,
+                        pages[pair * 2 + 1, c, h, rows, :].astype(jnp.float32),
+                        pages[pair * 2, c, h, rows, :].astype(jnp.float32),
+                    )
+                    mean = jnp.mean(wide * wide, -1, keepdims=True)
+                    at = (c * 2 + h) * page.shape[1]
+                    into = pl.ds(pl.multiple_of(at + i * 16, 16), 16)
+                    normed[into, :] = (wide * lax.rsqrt(mean + norm_eps) * gain[...]).astype(
+                        jnp.bfloat16
+                    )
+                    return carry
+
+                lax.fori_loop(0, page.shape[1] // 16, norm, 0)
+
+        def multiply(i, total):
+            part = pl.ds(pl.multiple_of(i * per_step, per_step), per_step)
+            slabs = weights[pl.ds(i * (per_step // depth), per_step // depth)]
+            return total + jnp.dot(
+                normed[:, part],
+                slabs.reshape(per_step, slab.shape[3]),
+                preferred_element_type=jnp.float32,
+            )
+
+        projected = lax.fori_loop(
+            0, 4, multiply, jnp.zeros((pair_count, slab.shape[3]), jnp.float32)
+        )
+        start_column = jnp.concatenate(columns, 0)
+        rows = pl.ds(pl.multiple_of(pair * pair_count, pair_count), pair_count)
+        first = block * queries.shape[0] + pair * pair_count
+        position = first + lax.broadcasted_iota(jnp.int32, (pair_count, 1), 0)
+        begin = start_column.astype(jnp.int32)
+        starts[rows, :] = begin
+        angles = (position - begin).astype(jnp.float32) * freq[...]
+        cosine, sine = jnp.cos(angles), jnp.sin(angles)
+        for head in range(query_width // HEAD_SIZE):
+            part = slice(head * HEAD_SIZE, (head + 1) * HEAD_SIZE)
+            queries[rows, part] = rotated(projected[:, part], cosine, sine)
+        keys[rows, :] = rotated(
+            projected[:, query_width : query_width + HEAD_SIZE], cosine, sine
+        )
+        values[rows, :] = projected[:, query_width + HEAD_SIZE :].astype(jnp.bfloat16)
+
+    def pick_sinks():
+        found = seg_starts()
+        count = NSEG * SINKS
+
+        def spread_out(shape, axis):
+            place = lax.broadcasted_iota(jnp.int32, shape, axis)
+            begin = jnp.zeros(shape, jnp.float32)
+            for segment in range(NSEG):
+                inside = (place >= segment * SINKS) & (place < (segment + 1) * SINKS)
+                begin = jnp.where(inside, found[segment], begin)
+            begin = begin.astype(jnp.int32)
+            return begin, begin + place % SINKS
+
+        begin, place = spread_out((1, count), 1)
+        sink_rows[0:1, :] = place
+        sink_rows[1:2, :] = begin
+        place = spread_out((count, 1), 0)[1] - block * queries.shape[0]
+        chosen = lax.broadcasted_iota(jnp.int32, (count, queries.shape[0]), 1) == place
+        chosen = chosen.astype(jnp.float32).astype(jnp.bfloat16)
+        for i, source in enumerate((keys, values)):
+            sink_pairs[i] = jnp.dot(
+                chosen, source[...], preferred_element_type=jnp.float32
+            ).astype(jnp.bfloat16)
+
     own_copies = [
         pltpu.make_async_copy(page, pages.at[z, core], local.at[0]),
         pltpu.make_async_copy(slab, weights.at[x * 4 + y], local.at[1]),
@@ -170,39 +284,60 @@
             for d in (1, -1):
                 arrived(("w2r", order, k, d), origin(order, k, -2 * d).at[0 if d == 1 else 1])
     page_step(1, 1)
-    for s, h in ((2, 0), (2, 1), (3, 0), (3, 1)):
-        page_step(s, h)
-    for h in range(2):
-        arrived(("c", 0, 0, h), page_at(0, h, 1 - core))
-    for s in range(4):
+
+    def passed(s):
         for h in range(2):
             for d in (1, -1):
                 if s < 3 or h == (0 if d == 1 else 1):
                     arrived(("c", d, s, h), page_at(-d * (s + 1), h, 1 - core))
+
+    own_copies[0].wait()
+    own_copies[1].wait()
+    for h in range(2):
+        arrived(("c", 0, 0, h), page_at(0, h, 1 - core))
+    passed(0)
+    project(0)
+    page_step(2, 0)
+    passed(1)
+    project(3 - 2 * dp)
+    page_step(2, 1)
+    passed(2)
+    project(1 + 2 * dp)
+    page_step(3, 0)
+    page_step(3, 1)
+    passed(3)
+    project(2)
+    pick_sinks()
     for c in started:
         c.wait_send()
-    own_copies[0].wait()
-    own_copies[1].wait()
 
 
 COPIES = 7 + 3 + 3 + 14 + 16 + 4 + 4 + 16 + 16
 
 
-def gather(page, slab, note):
+def gather(page, slab, note, gain, freq):
     rows, width = page.shape
     depth, columns = slab.shape
+    block_rows = KEY_VALUE_HEADS * rows
     vmem = pl.BlockSpec(memory_space=pltpu.VMEM)
-    hbm = pl.BlockSpec(memory_space=pltpu.HBM)
+    head_rows = jax.ShapeDtypeStruct((block_rows, HEAD_SIZE), page.dtype)
     return pl.pallas_call(
         gather_kernel,
         out_shape=(
-            jax.ShapeDtypeStruct((8, 2, 2, rows // 2, width), page.dtype),
-            jax.ShapeDtypeStruct((16, 2, 2, depth // 4, columns), slab.dtype),
-            jax.ShapeDtypeStruct((4, 4, 8, 1, note.shape[0]), note.dtype),
+            jax.ShapeDtypeStruct((block_rows, columns - 2 * HEAD_SIZE), page.dtype),
+            head_rows,
+            head_rows,
+            jax.ShapeDtypeStruct((block_rows, 1), jnp.int32),
+            jax.ShapeDtypeStruct((2, NSEG * SINKS), jnp.int32),
+            jax.ShapeDtypeStruct((2, NSEG * SINKS, HEAD_SIZE), page.dtype),
         ),
-        in_specs=[vmem] * 3,
-        out_specs=(hbm,) * 3,
+        in_specs=[vmem] * 5,
+        out_specs=(vmem,) * 6,
         scratch_shapes=[
+            pltpu.VMEM((8, 2, 2, rows // 2, width), page.dtype),
+            pltpu.VMEM((16, 2, 2, depth // 4, columns), slab.dtype),
+            pltpu.VMEM((4, 4, 8, 1, note.shape[0]), note.dtype),
+            pltpu.VMEM((2 * rows, width), page.dtype),
             pltpu.SemaphoreType.DMA((COPIES,)),
             pltpu.SemaphoreType.DMA((COPIES,)),
             pltpu.SemaphoreType.DMA((3,)),
@@ -213,6 +348,8 @@
         page.reshape(2, rows // 2, width),
         slab.reshape(2, 2, depth // 4, columns),
         note.reshape(1, -1),
+        gain.reshape(1, -1),
+        freq.reshape(1, -1),
     )
 
 
@@ -499,65 +636,12 @@
 
 def body(tokens, norm_gain, segments, deal_table, projection):
     group_id = lax.axis_index("dp")
-    device_number = lax.axis_index("tensor")
-    token_per_device = tokens.shape[1]
-    model_width = tokens.shape[2]
-    block_length = KEY_VALUE_HEADS * token_per_device
-    block_number = device_number // KEY_VALUE_HEADS
-    group_queries = QUERY_HEADS // KEY_VALUE_HEADS
-    own_page = tokens[0]
     owner_group = jnp.sum(jnp.where(jnp.arange(deal_table.shape[1]) == group_id, deal_table[0], 0))
-    stay_here = owner_group == group_id
-    widened = own_page.astype(jnp.float32)
-    normed = (
-        widened * lax.rsqrt(jnp.mean(widened * widened, -1, keepdims=True) + norm_eps) * norm_gain
-    ).astype(jnp.bfloat16)
-    client = jnp.where(stay_here, group_id, 1 - group_id).astype(jnp.int32)
+    client = jnp.where(owner_group == group_id, group_id, 1 - group_id).astype(jnp.int32)
     note = jnp.concatenate((segments[0], jnp.broadcast_to(client, segments[0].shape)))
-    pages, weights, notes = gather(normed, projection, note)
-    weights_held = weights.reshape(model_width, projection.shape[1])
-    notes = notes.reshape(4, 4, KEY_VALUE_HEADS, 2, token_per_device).transpose(1, 0, 2, 3, 4)
-    notes = notes.reshape(-1, KEY_VALUE_HEADS, 2, token_per_device)
-    counts_int = jnp.sum(
-        (notes[:, :, 0, :, None] == jnp.arange(NSEG)).astype(jnp.int32), (0, 1, 2)
-    )
-    seg_starts = jnp.cumsum(counts_int) - counts_int
-    own_notes = lax.dynamic_index_in_dim(notes, block_number, 0, keepdims=False)
-    segment_match = own_notes[:, 0].reshape(block_length)[:, None] == jnp.arange(NSEG)[None, :]
-    starts_block = jnp.sum(jnp.where(segment_match, seg_starts[None, :], 0), 1)
-    clients = own_notes[:, 1, 0].reshape(4, 2, 1, 1)
-    pages = pages.reshape(4, 2, 2, token_per_device, model_width)
-    rows_block = jnp.where(clients == 1, pages[:, 1], pages[:, 0]).reshape(
-        block_length, model_width
-    )
-    projected = jnp.dot(rows_block, weights_held, preferred_element_type=jnp.float32)
     rope_freq = rope_base ** (-(jnp.arange(0, HEAD_SIZE, 2).astype(jnp.float32) / HEAD_SIZE))
-    block_positions = block_number * block_length + jnp.arange(block_length)
-    angles = (block_positions - starts_block).astype(jnp.float32)[:, None] * rope_freq[None, :]
-    queries = rotary(
-        projected[:, : group_queries * HEAD_SIZE].reshape(block_length, group_queries, HEAD_SIZE),
-        angles[:, None, :],
-    ).astype(jnp.bfloat16)
-    keys_own = rotary(
-        projected[:, group_queries * HEAD_SIZE : (group_queries + 1) * HEAD_SIZE], angles
-    ).astype(jnp.bfloat16)
-    values_own = projected[:, (group_queries + 1) * HEAD_SIZE :].astype(jnp.bfloat16)
-    local_pairs = jnp.stack((keys_own, values_own))
-    sink_positions = (seg_starts[:, None] + jnp.arange(SINKS)[None, :]).reshape(NSEG * SINKS)
-    local_rows = sink_positions - block_number * block_length
-    selector = (local_rows[:, None] == jnp.arange(block_length)[None, :]).astype(jnp.bfloat16)
-    sink_pairs = jnp.einsum(
-        "sr,prd->psd", selector, local_pairs, preferred_element_type=jnp.float32
-    ).astype(jnp.bfloat16)
-    sink_rows = jnp.stack((sink_positions, jnp.repeat(seg_starts, SINKS)))
-    contexts, key_cache, value_cache = attend_pages(
-        queries.reshape(block_length, group_queries * HEAD_SIZE),
-        keys_own,
-        values_own,
-        starts_block[:, None],
-        sink_rows,
-        sink_pairs,
-    )
+    attended = gather(tokens[0], projection, note, norm_gain, rope_freq)
+    contexts, key_cache, value_cache = attend_pages(*attended)
     context = jnp.where(owner_group == 1, contexts[1], contexts[0])
     return (context[None], key_cache[None], value_cache[None])
 

time: 216 us -> 185 us (0.86)
  other arithmetic: 23.9 us -> 4.49 us
  local copies, waits for them, and re-layouts: 13.3 us -> 2.63 us
  matrix products: 9.96 us -> 0 us
  Pallas kernels: 166 us -> 175 us
    dot_general x2 -> x0, matrix products: 9.96 us -> none  [the longest x1 9.08 us: body(): jnp.dot(rows_block, weights_held, preferred_element_type=jnp.float32)]
    pallas_call x1, Pallas kernels: 93.7 us -> 101 us  [gather(): pl.pallas_call(gather_kernel, out_shape=(jax.ShapeDtypeStruct((block_rows...]
    select_n x1 -> x0, other arithmetic: 6.62 us -> none  [body(): jnp.where(clients == 1, pages[:, 1], pages[:, 0])]
    another operation x4 -> x0, other arithmetic: 6.44 us -> none
    unnamed x16 -> x6, local copies, waits for them, and re-layouts: 7.47 us -> 1.41 us
    convert_element_type x2 -> x0, other arithmetic: 2.56 us -> none  [the longest x1 2.55 us: body(): normed = (widened * lax.rsqrt(jnp.mean(widened * widened, -1, keepdims=Tr...]
    concatenate x2 -> x0, other arithmetic: 2.27 us -> none  [rotary(): jnp.concatenate((first_half * cosine - second_half * sine_part, second_ha...]
    slice x4 -> x0, local copies, waits for them, and re-layouts: 2.17 us -> none  [the longest x2 1.91 us: rotary(): second_half = values[..., half_width:]]
where the time goes in v5:
time: 185 us; the launch traced here: 184 us
  Pallas kernels  175 us (95%)
  other arithmetic  4.49 us (2%)
  local copies, waits for them, and re-layouts  2.63 us (1%)
  between operations  1.97 us (1%)
    pallas_call x1, Pallas kernels, gather(): pl.pallas_call(gather_kernel, out_shape=(jax.ShapeDtypeStruct((block_rows...  101 us
    pallas_call x1, Pallas kernels, attend_pages(): pl.pallas_call(attend_kernel, out_shape=(jax.ShapeDtypeStruct((2, PAGE_RO...  73.9 us

profile of v5, /device:TPU:32, one launch (start us, length us, event | category | flops | bytes accessed | tf_op | source)
XLA Modules:
  0.0 184.2 jit_solution(11943598735315792007)
XLA Ops:
  0.6 1.3 fusion
  3.2 1.2 concatenate.3
  4.5 0.5 negate_power_fusion.freq
  5.0 101.2 %gather.1 = (bf16[1024,512]{1,0:T(8,128)(2,1)}, bf16[1024,128]{1,0:T(8,128)(2,1)}, bf16[1024,128]{1,0:T(8,128)(2,1)}, s32[1024,1]{1,0:T(8,128)}, s32[2,32]{1,0:T(2,128)}, /*index=5*/bf16[2,32,128]{2,1,0:T(8,128)(2,1)}) custom-call(bf16[2,64,4096]{2,1,0:T(8,128)(2,1)} %bitcast.9, bf16[2,2,64,768]{3,2,1,0:T(8,128)(2,1)} %bitcast.10, s32[1,256]{1,0:T(1,128)} %bitcast.14, ...), custom_call_target="tpu_custom_call" | custom-call | tf_op jit(solution)/shard_map/gather/pallas_call | solution.py:324
  106.2 73.9 %attend.1 = (bf16[2,128,4096]{2,1,0:T(8,128)(2,1)}, bf16[8,128,128]{2,1,0:T(8,128)(2,1)}, bf16[8,128,128]{2,1,0:T(8,128)(2,1)}) custom-call(bf16[1024,512]{1,0:T(8,128)(2,1)} %get-tuple-element.12.queries, bf16[1024,128]{1,0:T(8,128)(2,1)} %get-tuple-element.13.keys, bf16[1024,128]{1,0:T(8,128)(2,1)} %get-tuple-element.14.values, ...), custom_call_target="tpu_custom_call" | custom-call | tf_op jit(solution)/shard_map/attend/pallas_call | solution.py:613
  180.1 0.0 copy-start.1
  180.1 0.0 copy-start
  180.1 2.7 %slice_select_fusion = bf16[1,128,4096]{2,1,0:T(8,128)(2,1)} fusion(bf16[2,128,4096]{2,1,0:T(8,128)(2,1)} %get-tuple-element.18, pred[]{:T(512)S(6)} %eq.14), kind=kLoop, calls=%fused_computation | loop fusion | flops 524288 | bytes 3145729 | tf_op jit(solution)/shard_map/jit(_where)/select_n | solution.py:645
  182.8 0.0 copy-done.1
  182.8 0.7 copy.10
  183.5 0.0 copy-done
  183.5 0.7 copy.11
Async XLA Ops:
  180.1 2.7 %copy-start.1 = (bf16[8,128,128]{2,1,0:T(8,128)(2,1)S(1)}, bf16[8,128,128]{2,1,0:T(8,128)(2,1)}, u32[]{:S(2)}) copy-start(bf16[8,128,128]{2,1,0:T(8,128)(2,1)} %get-tuple-element.19) | copy-start | bytes 786436
  180.1 3.4 %copy-start = (bf16[8,128,128]{2,1,0:T(8,128)(2,1)S(1)}, bf16[8,128,128]{2,1,0:T(8,128)(2,1)}, u32[]{:S(2)}) copy-start(bf16[8,128,128]{2,1,0:T(8,128)(2,1)} %get-tuple-element.20) | copy-start | bytes 786436

commit v6 on v5

--- a/solution.py
+++ b/solution.py
@@ -17,26 +17,57 @@
 norm_eps = 1e-05
 
 
-def gather_kernel(
+def kernel(
     page,
     slab,
     note,
     gain,
     freq,
-    queries,
-    keys,
-    values,
-    starts,
-    sink_rows,
-    sink_pairs,
+    context,
+    key_out,
+    value_out,
     pages,
     weights,
     notes,
     normed,
+    queries,
+    starts,
+    sink_rows,
+    sink_pairs,
+    key_window,
+    value_window,
+    sinks,
+    mixed,
+    passing,
     send,
     recv,
     local,
+    send_mixed,
+    recv_mixed,
+    local_mixed,
 ):
+    keys = key_window.at[pl.ds(WINDOW, queries.shape[0])]
+    values = value_window.at[pl.ds(WINDOW, queries.shape[0])]
+    meet()
+    send_cache, send_edges, attend_all = attention(
+        queries,
+        keys,
+        values,
+        starts,
+        sink_rows,
+        sink_pairs,
+        context,
+        key_out,
+        value_out,
+        key_window,
+        value_window,
+        sinks,
+        mixed,
+        passing,
+        send_mixed,
+        recv_mixed,
+        local_mixed,
+    )
     dp = lax.axis_index("dp")
     t = lax.axis_index("tensor")
     core, zh = t % 2, (t // 2) % 4
@@ -78,12 +109,6 @@
     columns = [device(r, 0, z, core) for r in range(1, 4)]
     lines = [device(0, r, z, core) for r in range(1, 4)]
     ring = {1: device(0, 0, z + 1, core), -1: device(0, 0, z + 7, core)}
-    barrier = pltpu.get_barrier_semaphore()
-    peers = group + columns + lines + [ring[1], ring[-1]]
-    for peer in peers:
-        pl.semaphore_signal(barrier, inc=1, device_id=peer, device_id_type=pl.DeviceIdType.MESH)
-    pl.semaphore_wait(barrier, len(peers))
-
     def page_at(dz, h, c):
         return pages.at[(z + dz + 8) % 8, c, h]
 
@@ -301,56 +326,23 @@
     passed(1)
     project(3 - 2 * dp)
     page_step(2, 1)
+    send_cache(0)
+    send_cache(3 - 2 * dp)
     passed(2)
     project(1 + 2 * dp)
     page_step(3, 0)
     page_step(3, 1)
+    send_cache(1 + 2 * dp)
     passed(3)
-    project(2)
+    project(FAR)
     pick_sinks()
+    send_edges()
+    attend_all()
     for c in started:
         c.wait_send()
 
 
 COPIES = 7 + 3 + 3 + 14 + 16 + 4 + 4 + 16 + 16
-
-
-def gather(page, slab, note, gain, freq):
-    rows, width = page.shape
-    depth, columns = slab.shape
-    block_rows = KEY_VALUE_HEADS * rows
-    vmem = pl.BlockSpec(memory_space=pltpu.VMEM)
-    head_rows = jax.ShapeDtypeStruct((block_rows, HEAD_SIZE), page.dtype)
-    return pl.pallas_call(
-        gather_kernel,
-        out_shape=(
-            jax.ShapeDtypeStruct((block_rows, columns - 2 * HEAD_SIZE), page.dtype),
-            head_rows,
-            head_rows,
-            jax.ShapeDtypeStruct((block_rows, 1), jnp.int32),
-            jax.ShapeDtypeStruct((2, NSEG * SINKS), jnp.int32),
-            jax.ShapeDtypeStruct((2, NSEG * SINKS, HEAD_SIZE), page.dtype),
-        ),
-        in_specs=[vmem] * 5,
-        out_specs=(vmem,) * 6,
-        scratch_shapes=[
-            pltpu.VMEM((8, 2, 2, rows // 2, width), page.dtype),
-            pltpu.VMEM((16, 2, 2, depth // 4, columns), slab.dtype),
-            pltpu.VMEM((4, 4, 8, 1, note.shape[0]), note.dtype),
-            pltpu.VMEM((2 * rows, width), page.dtype),
-            pltpu.SemaphoreType.DMA((COPIES,)),
-            pltpu.SemaphoreType.DMA((COPIES,)),
-            pltpu.SemaphoreType.DMA((3,)),
-        ],
-        compiler_params=pltpu.CompilerParams(collective_id=0, has_side_effects=True),
-        name="gather",
-    )(
-        page.reshape(2, rows // 2, width),
-        slab.reshape(2, 2, depth // 4, columns),
-        note.reshape(1, -1),
-        gain.reshape(1, -1),
-        freq.reshape(1, -1),
-    )
 
 
 PAGE_ROWS = 128
@@ -360,7 +352,20 @@
 FAR = 2
 
 
-def attend_kernel(
+def meet():
+    dp = lax.axis_index("dp")
+    t = lax.axis_index("tensor")
+    q, block = t % 8, t // 8
+    peers = [(dp, block * 8 + (q + r) % 8) for r in range(1, 8)]
+    peers += [(dp, ((block + r) % 16) * 8 + q) for r in range(1, 16)]
+    peers += [(1 - dp, block * 8 + (q + r) % 8) for r in range(8)]
+    barrier = pltpu.get_barrier_semaphore()
+    for peer in peers:
+        pl.semaphore_signal(barrier, inc=1, device_id=peer, device_id_type=pl.DeviceIdType.MESH)
+    pl.semaphore_wait(barrier, len(peers))
+
+
+def attention(
     queries,
     keys,
     values,
@@ -395,51 +400,26 @@
             device_id_type=pl.DeviceIdType.MESH,
         )
 
-    def head(r):
-        return (dp, block * 8 + (q + r) % 8)
+    def plane(r):
+        return (dp, ((block + r) % 16) * 8 + q)
 
     def page_near(shift, flip):
         return ((zh + shift) % 4) * 2 + (core + flip) % 2
 
     partner = (1 - dp, t)
-
-    def plane(r):
-        return (dp, ((block + r) % 16) * 8 + q)
-
-    peers = [head(r) for r in range(1, 8)] + [plane(r) for r in range(1, 16)]
-    peers += [(1 - dp, block * 8 + (q + r) % 8) for r in range(8)]
-    barrier = pltpu.get_barrier_semaphore()
-    for peer in peers:
-        pl.semaphore_signal(barrier, inc=1, device_id=peer, device_id_type=pl.DeviceIdType.MESH)
-    pl.semaphore_wait(barrier, len(peers))
-
-    own_rows = pl.ds(WINDOW, keys.shape[0])
     last_rows = pl.ds(keys.shape[0] - WINDOW, WINDOW)
     first_rows = pl.ds(0, WINDOW)
 
     def page_rows(page):
         return pl.ds(pl.multiple_of(page * PAGE_ROWS, PAGE_ROWS), PAGE_ROWS)
 
-    at = CONTEXT_COPIES
     sent = []
-    for i, (source, target) in enumerate(((keys, key_window), (values, value_window))):
-        c = copy(at + i, source.at[last_rows], target.at[first_rows], plane(1))
-        c.start()
-        sent.append(c)
-    at += 2
-    for r in range(1, 16):
-        c = copy(at + r - 1, sink_pairs, sinks.at[block], plane(r))
-        c.start()
-        sent.append(c)
-    locals_now = [
-        pltpu.make_async_copy(keys, key_window.at[own_rows], local.at[0]),
-        pltpu.make_async_copy(values, value_window.at[own_rows], local.at[1]),
-        pltpu.make_async_copy(sink_pairs, sinks.at[block], local.at[2]),
-        pltpu.make_async_copy(keys.at[page_rows(q)], key_out.at[q], local.at[3]),
-        pltpu.make_async_copy(values.at[page_rows(q)], value_out.at[q], local.at[4]),
+    own_copies = [
+        pltpu.make_async_copy(sink_pairs, sinks.at[block], local.at[0]),
+        pltpu.make_async_copy(keys.at[page_rows(q)], key_out.at[q], local.at[1]),
+        pltpu.make_async_copy(values.at[page_rows(q)], value_out.at[q], local.at[2]),
     ]
-    for c in locals_now:
-        c.start()
+    edge_slot, sink_slot = CONTEXT_COPIES, CONTEXT_COPIES + 2
     caches = ((keys, key_out), (values, value_out))
     spread = [(shift, flip) for shift in (FAR, 3, 1, 0) for flip in (1, 0)][:7]
 
@@ -449,189 +429,235 @@
     def passing_slot(flip, i):
         return CONTEXT_COPIES + 33 + flip * 2 + i
 
-    for shift, flip in spread:
-        page = page_near(shift, flip)
-        for i, (source, target) in enumerate(caches):
-            piece = source.at[page_rows(page)]
-            if shift == FAR:
-                c = copy(
-                    passing_slot(flip, i), piece, passing.at[i, flip], (1 - dp, block * 8 + page)
-                )
-            else:
-                c = copy(cache_slot(shift, flip, i), piece, target.at[q], (dp, block * 8 + page))
+    def send_cache(shift):
+        own = isinstance(shift, int) and shift == 0
+        far = isinstance(shift, int) and shift == FAR
+        for flip in (1,) if own else (1, 0):
+            page = page_near(shift, flip)
+            for i, (source, target) in enumerate(caches):
+                piece = source.at[page_rows(page)]
+                if far:
+                    c = copy(
+                        passing_slot(flip, i),
+                        piece,
+                        passing.at[i, flip],
+                        (1 - dp, block * 8 + page),
+                    )
+                else:
+                    c = copy(
+                        cache_slot(shift, flip, i), piece, target.at[q], (dp, block * 8 + page)
+                    )
+                c.start()
+                sent.append(c)
+
+    def send_edges():
+        for i, (source, target) in enumerate(((keys, key_window), (values, value_window))):
+            c = copy(
+                edge_slot + i, source.at[last_rows], target.at[first_rows], plane(1)
+            )
             c.start()
             sent.append(c)
+        send_cache(FAR)
+        for c in own_copies[1:]:
+            c.start()
+        for r in range(1, 16):
+            c = copy(sink_slot + r - 1, sink_pairs, sinks.at[block], plane(r))
+            c.start()
+            sent.append(c)
+        own_copies[0].start()
 
     def hand_on(flip, i):
         piece = passing.at[i, flip]
         source = page_near(4 - FAR, flip)
         return copy(cache_slot(FAR, flip, i), piece, caches[i][1].at[source], partner)
 
-    at = CONTEXT_COPIES
-    for i, target in enumerate((key_window, value_window)):
-        copy(at + i, target.at[first_rows], target.at[first_rows], plane(1)).wait_recv()
-    at += 2
-    for r in range(1, 16):
-        landed = sinks.at[(block + 16 - r) % 16]
-        copy(at + r - 1, landed, landed, plane(1)).wait_recv()
-    for c in locals_now[:3]:
-        c.wait()
-
-    sink_sum = jnp.sum(sinks[...].astype(jnp.float32), 0).astype(jnp.bfloat16)
-    sink_keys, sink_values = sink_sum[0], sink_sum[1]
-    scale = HEAD_SIZE ** (-0.5)
-    last_dims = (((1,), (1,)), ((), ()))
-
-    def page_of(step):
-        turn = step // 2
-        return page_near(FAR + turn * (turn + 1) // 2, 1 + step)
-
-    def columns(head_index):
-        return pl.ds(pl.multiple_of(head_index * width, width), width)
-
-    def to_half(step, half):
-        target = context.at[dp, :, columns(q)]
-        i = step if half == 0 else 8 + step
-        side = dp if half == 0 else 1 - dp
-        return copy(i, mixed.at[step], target, (side, block * 8 + page_of(step)))
-
-    def attend(step, carry):
-        page = page_of(step)
-        rows = page_rows(page)
-        row_start = starts[rows, :]
-        first = block * keys.shape[0] + page * PAGE_ROWS
-        query_pos = first + lax.broadcasted_iota(jnp.int32, (PAGE_ROWS, 1), 0)
-        key_pos = first - WINDOW + lax.broadcasted_iota(jnp.int32, (PAGE_ROWS, REACH), 1)
-        allowed = (
-            (key_pos <= query_pos) & (key_pos >= row_start) & (key_pos >= query_pos - WINDOW)
-        )
-        sink_pos = sink_rows[0:1, :]
-        sink_allowed = (
-            (sink_rows[1:2, :] == row_start)
-            & (sink_pos <= query_pos)
-            & (sink_pos < query_pos - WINDOW)
-        )
-        reach = pl.ds(pl.multiple_of(page * PAGE_ROWS, PAGE_ROWS), REACH)
-        near_keys = key_window[reach, :]
-        near_values = value_window[reach, :]
-        for h in range(width // HEAD_SIZE):
-            part = pl.ds(h * HEAD_SIZE, HEAD_SIZE)
-            query = queries[rows, part]
-            scores = (
-                lax.dot_general(query, near_keys, last_dims, preferred_element_type=jnp.float32)
-                * scale
+    def attend_all():
+        for i, target in enumerate((key_window, value_window)):
+            copy(edge_slot + i, target.at[first_rows], target.at[first_rows], plane(1)).wait_recv()
+        for r in range(1, 16):
+            landed = sinks.at[(block + 16 - r) % 16]
+            copy(sink_slot + r - 1, landed, landed, plane(1)).wait_recv()
+        own_copies[0].wait()
+
+        sink_sum = jnp.sum(sinks[...].astype(jnp.float32), 0).astype(jnp.bfloat16)
+        sink_keys, sink_values = sink_sum[0], sink_sum[1]
+        scale = HEAD_SIZE ** (-0.5)
+        last_dims = (((1,), (1,)), ((), ()))
+
+        def page_of(step):
+            turn = step // 2
+            return page_near(FAR + turn * (turn + 1) // 2, 1 + step)
+
+        def columns(head_index):
+            return pl.ds(pl.multiple_of(head_index * width, width), width)
+
+        def to_half(step, half):
+            target = context.at[dp, :, columns(q)]
+            i = step if half == 0 else 8 + step
+            side = dp if half == 0 else 1 - dp
+            return copy(i, mixed.at[step], target, (side, block * 8 + page_of(step)))
+
+        def attend(step, carry):
+            page = page_of(step)
+            rows = page_rows(page)
+            row_start = starts[rows, :]
+            first = block * keys.shape[0] + page * PAGE_ROWS
+            query_pos = first + lax.broadcasted_iota(jnp.int32, (PAGE_ROWS, 1), 0)
+            key_pos = first - WINDOW + lax.broadcasted_iota(jnp.int32, (PAGE_ROWS, REACH), 1)
+            allowed = (
+                (key_pos <= query_pos) & (key_pos >= row_start) & (key_pos >= query_pos - WINDOW)
             )
-            sink_scores = (
-                lax.dot_general(query, sink_keys, last_dims, preferred_element_type=jnp.float32)
-                * scale
+            sink_pos = sink_rows[0:1, :]
+            sink_allowed = (
+                (sink_rows[1:2, :] == row_start)
+                & (sink_pos <= query_pos)
+                & (sink_pos < query_pos - WINDOW)
             )
-            scores = jnp.where(allowed, scores, -jnp.inf)
-            sink_scores = jnp.where(sink_allowed, sink_scores, -jnp.inf)
-            top = jnp.maximum(
-                jnp.max(scores, -1, keepdims=True), jnp.max(sink_scores, -1, keepdims=True)
-            )
-            near = jnp.exp(scores - top)
-            far = jnp.exp(sink_scores - top)
-            inverse = 1.0 / (
-                jnp.sum(near, -1, keepdims=True) + jnp.sum(far, -1, keepdims=True)
-            )
-            result = jnp.dot(
-                (near * inverse).astype(jnp.bfloat16),
-                near_values,
-                preferred_element_type=jnp.float32,
-            ) + jnp.dot(
-                (far * inverse).astype(jnp.bfloat16),
-                sink_values,
-                preferred_element_type=jnp.float32,
-            )
-            mixed[step, :, part] = result.astype(jnp.bfloat16)
-
-        @pl.when(step > 0)
-        def _():
-            to_half(step - 1, 1).start()
-
-        @pl.when(step > 2)
-        def _():
-            to_half(step - 1, 0).start()
-
-        @pl.when(step == 2)
-        def _():
-            for flip in range(2):
-                for i in range(2):
-                    piece = passing.at[i, flip]
-                    copy(passing_slot(flip, i), piece, piece, partner).wait_recv()
-                    hand_on(flip, i).start()
-
-        return carry
-
-    lax.fori_loop(0, 8, attend, 0)
-    own = pltpu.make_async_copy(mixed.at[7], context.at[dp, :, columns(q)], local.at[5])
-    own.start()
-    to_half(7, 1).start()
-
-    def source_of(step):
-        turn = step // 2
-        return page_near(8 - FAR - turn * (turn + 1) // 2, 1 + step)
-
-    def landed(step, half):
-        return context.at[dp if half == 0 else 1 - dp, :, columns(source_of(step))]
-
-    def pass_context(step):
-        piece = landed(step, 1)
-        return copy(step, piece, piece, partner)
-
-    for step in range(2):
-        copy(8 + step, landed(step, 1), landed(step, 1), partner).wait_recv()
-        pass_context(step).start()
-    for shift, flip in spread:
-        source = page_near(4 - shift, flip)
-        for i in range(2):
-            piece = caches[i][1].at[source]
-            copy(cache_slot(shift, flip, i), piece, piece, partner).wait_recv()
-    for step in range(2, 8):
-        copy(8 + step, landed(step, 1), landed(step, 1), partner).wait_recv()
-    for step in range(7):
-        copy(step, landed(step, 0), landed(step, 0), partner).wait_recv()
-    for c in sent + [hand_on(flip, i) for flip in range(2) for i in range(2)]:
-        c.wait_send()
-    for c in locals_now[3:]:
-        c.wait()
-    for step in range(8):
-        if step < 2:
-            pass_context(step).wait_send()
-        elif step < 7:
-            to_half(step, 0).wait_send()
-        to_half(step, 1).wait_send()
-    own.wait()
-
-
-def attend_pages(queries, keys, values, starts, sink_rows, sink_pairs):
-    rows, width = queries.shape
+            reach = pl.ds(pl.multiple_of(page * PAGE_ROWS, PAGE_ROWS), REACH)
+            near_keys = key_window[reach, :]
+            near_values = value_window[reach, :]
+            for h in range(width // HEAD_SIZE):
+                part = pl.ds(h * HEAD_SIZE, HEAD_SIZE)
+                query = queries[rows, part]
+                scores = (
+                    lax.dot_general(query, near_keys, last_dims, preferred_element_type=jnp.float32)
+                    * scale
+                )
+                sink_scores = (
+                    lax.dot_general(query, sink_keys, last_dims, preferred_element_type=jnp.float32)
+                    * scale
+                )
+                scores = jnp.where(allowed, scores, -jnp.inf)
+                sink_scores = jnp.where(sink_allowed, sink_scores, -jnp.inf)
+                top = jnp.maximum(
+                    jnp.max(scores, -1, keepdims=True), jnp.max(sink_scores, -1, keepdims=True)
+                )
+                near = jnp.exp(scores - top)
+                far = jnp.exp(sink_scores - top)
+                inverse = 1.0 / (
+                    jnp.sum(near, -1, keepdims=True) + jnp.sum(far, -1, keepdims=True)
+                )
+                result = jnp.dot(
+                    (near * inverse).astype(jnp.bfloat16),
+                    near_values,
+                    preferred_element_type=jnp.float32,
+                ) + jnp.dot(
+                    (far * inverse).astype(jnp.bfloat16),
+                    sink_values,
+                    preferred_element_type=jnp.float32,
+                )
+                mixed[step, :, part] = result.astype(jnp.bfloat16)
+
+            @pl.when(step > 0)
+            def _():
+                to_half(step - 1, 1).start()
+
+            @pl.when(step > 2)
+            def _():
+                to_half(step - 1, 0).start()
+
+            @pl.when(step == 2)
+            def _():
+                for flip in range(2):
+                    for i in range(2):
+                        piece = passing.at[i, flip]
+                        copy(passing_slot(flip, i), piece, piece, partner).wait_recv()
+                        hand_on(flip, i).start()
+
+            return carry
+
+        lax.fori_loop(0, 8, attend, 0)
+        own = pltpu.make_async_copy(mixed.at[7], context.at[dp, :, columns(q)], local.at[3])
+        own.start()
+        to_half(7, 1).start()
+
+        def source_of(step):
+            turn = step // 2
+            return page_near(8 - FAR - turn * (turn + 1) // 2, 1 + step)
+
+        def landed(step, half):
+            return context.at[dp if half == 0 else 1 - dp, :, columns(source_of(step))]
+
+        def pass_context(step):
+            piece = landed(step, 1)
+            return copy(step, piece, piece, partner)
+
+        for step in range(2):
+            copy(8 + step, landed(step, 1), landed(step, 1), partner).wait_recv()
+            pass_context(step).start()
+        for shift, flip in spread:
+            source = page_near(4 - shift, flip)
+            for i in range(2):
+                piece = caches[i][1].at[source]
+                copy(cache_slot(shift, flip, i), piece, piece, partner).wait_recv()
+        for step in range(2, 8):
+            copy(8 + step, landed(step, 1), landed(step, 1), partner).wait_recv()
+        for step in range(7):
+            copy(step, landed(step, 0), landed(step, 0), partner).wait_recv()
+        for c in sent + [hand_on(flip, i) for flip in range(2) for i in range(2)]:
+            c.wait_send()
+        for c in own_copies[1:]:
+            c.wait()
+        for step in range(8):
+            if step < 2:
+                pass_context(step).wait_send()
+            elif step < 7:
+                to_half(step, 0).wait_send()
+            to_half(step, 1).wait_send()
+        own.wait()
+
+    return send_cache, send_edges, attend_all
+
+
+def mixed_pages(page, slab, note, gain, freq):
+    rows, features = page.shape
+    depth, columns = slab.shape
+    block_rows = KEY_VALUE_HEADS * rows
+    width = columns - 2 * HEAD_SIZE
+    count = NSEG * SINKS
     vmem = pl.BlockSpec(memory_space=pltpu.VMEM)
     hbm = pl.BlockSpec(memory_space=pltpu.HBM)
-    cache = jax.ShapeDtypeStruct((KEY_VALUE_HEADS, PAGE_ROWS, HEAD_SIZE), keys.dtype)
+    cache = jax.ShapeDtypeStruct((KEY_VALUE_HEADS, PAGE_ROWS, HEAD_SIZE), page.dtype)
+    dtype = page.dtype
     return pl.pallas_call(
-        attend_kernel,
+        kernel,
         out_shape=(
-            jax.ShapeDtypeStruct((2, PAGE_ROWS, KEY_VALUE_HEADS * width), queries.dtype),
+            jax.ShapeDtypeStruct((2, PAGE_ROWS, KEY_VALUE_HEADS * width), dtype),
             cache,
             cache,
         ),
-        in_specs=[vmem] * 6,
+        in_specs=[vmem] * 5,
         out_specs=(hbm,) * 3,
         scratch_shapes=[
-            pltpu.VMEM((WINDOW + rows, HEAD_SIZE), keys.dtype),
-            pltpu.VMEM((WINDOW + rows, HEAD_SIZE), keys.dtype),
-            pltpu.VMEM((16,) + sink_pairs.shape, sink_pairs.dtype),
-            pltpu.VMEM((8, PAGE_ROWS, width), queries.dtype),
-            pltpu.VMEM((2, 2, PAGE_ROWS, HEAD_SIZE), keys.dtype),
+            pltpu.VMEM((8, 2, 2, rows // 2, features), dtype),
+            pltpu.VMEM((16, 2, 2, depth // 4, columns), slab.dtype),
+            pltpu.VMEM((4, 4, 8, 1, note.shape[0]), note.dtype),
+            pltpu.VMEM((2 * rows, features), dtype),
+            pltpu.VMEM((block_rows, width), dtype),
+            pltpu.VMEM((block_rows, 1), jnp.int32),
+            pltpu.VMEM((2, count), jnp.int32),
+            pltpu.VMEM((2, count, HEAD_SIZE), dtype),
+            pltpu.VMEM((WINDOW + block_rows, HEAD_SIZE), dtype),
+            pltpu.VMEM((WINDOW + block_rows, HEAD_SIZE), dtype),
+            pltpu.VMEM((16, 2, count, HEAD_SIZE), dtype),
+            pltpu.VMEM((8, PAGE_ROWS, width), dtype),
+            pltpu.VMEM((2, 2, PAGE_ROWS, HEAD_SIZE), dtype),
+            pltpu.SemaphoreType.DMA((COPIES,)),
+            pltpu.SemaphoreType.DMA((COPIES,)),
+            pltpu.SemaphoreType.DMA((3,)),
             pltpu.SemaphoreType.DMA((ATTEND_COPIES,)),
             pltpu.SemaphoreType.DMA((ATTEND_COPIES,)),
-            pltpu.SemaphoreType.DMA((6,)),
+            pltpu.SemaphoreType.DMA((4,)),
         ],
-        compiler_params=pltpu.CompilerParams(collective_id=1, has_side_effects=True),
-        name="attend",
-    )(queries, keys, values, starts, sink_rows, sink_pairs)
+        compiler_params=pltpu.CompilerParams(collective_id=0, has_side_effects=True),
+        name="mixed_pages",
+    )(
+        page.reshape(2, rows // 2, features),
+        slab.reshape(2, 2, depth // 4, columns),
+        note.reshape(1, -1),
+        gain.reshape(1, -1),
+        freq.reshape(1, -1),
+    )
 
 
 def body(tokens, norm_gain, segments, deal_table, projection):
@@ -640,8 +666,9 @@
     client = jnp.where(owner_group == group_id, group_id, 1 - group_id).astype(jnp.int32)
     note = jnp.concatenate((segments[0], jnp.broadcast_to(client, segments[0].shape)))
     rope_freq = rope_base ** (-(jnp.arange(0, HEAD_SIZE, 2).astype(jnp.float32) / HEAD_SIZE))
-    attended = gather(tokens[0], projection, note, norm_gain, rope_freq)
-    contexts, key_cache, value_cache = attend_pages(*attended)
+    contexts, key_cache, value_cache = mixed_pages(
+        tokens[0], projection, note, norm_gain, rope_freq
+    )
     context = jnp.where(owner_group == 1, contexts[1], contexts[0])
     return (context[None], key_cache[None], value_cache[None])
 

time: 185 us -> 180 us (0.973)
  Pallas kernels: 175 us -> 170 us
    pallas_call x2 -> x1, Pallas kernels: 175 us -> 170 us  [mixed_pages(): pl.pallas_call(kernel, out_shape=(jax.ShapeDtypeStruct((2, PAGE_ROWS, KEY...]
where the time goes in v6:
time: 180 us; the launch traced here: 179 us
  Pallas kernels  170 us (94%)
  other arithmetic  4.49 us (2%)
  local copies, waits for them, and re-layouts  2.63 us (1%)
  between operations  1.96 us (1%)
    pallas_call x1, Pallas kernels, mixed_pages(): pl.pallas_call(kernel, out_shape=(jax.ShapeDtypeStruct((2, PAGE_ROWS, KEY...  170 us

profile of v6, /device:TPU:32, one launch (start us, length us, event | category | flops | bytes accessed | tf_op | source)
XLA Modules:
  0.0 179.1 jit_solution(3411031140381570471)
XLA Ops:
  0.6 1.3 fusion
  3.2 1.2 concatenate.3
  4.5 0.5 negate_power_fusion.freq
  5.0 170.0 %mixed_pages.1 = (bf16[2,128,4096]{2,1,0:T(8,128)(2,1)}, bf16[8,128,128]{2,1,0:T(8,128)(2,1)}, bf16[8,128,128]{2,1,0:T(8,128)(2,1)}) custom-call(bf16[2,64,4096]{2,1,0:T(8,128)(2,1)} %bitcast.9, bf16[2,2,64,768]{3,2,1,0:T(8,128)(2,1)} %bitcast.10, s32[1,256]{1,0:T(1,128)} %bitcast.14, f32[1,4096]{1,0:T(1,128)} %bitcast.13, f32[1,64]{1,0:T(1,128)} %negate_power_fusion.freq), custom_call_target="tpu_custom_call" | custom-call | tf_op jit(solution)/shard_map/mixed_pages/pallas_call | solution.py:622
  175.0 0.0 copy-start.1
  175.0 0.0 copy-start
  175.0 2.7 %slice_select_fusion = bf16[1,128,4096]{2,1,0:T(8,128)(2,1)} fusion(bf16[2,128,4096]{2,1,0:T(8,128)(2,1)} %get-tuple-element.6, pred[]{:T(512)S(6)} %eq.14), kind=kLoop, calls=%fused_computation | loop fusion | flops 524288 | bytes 3145729 | tf_op jit(solution)/shard_map/jit(_where)/select_n | solution.py:672
  177.7 0.0 copy-done.1
  177.7 0.7 copy.10
  178.4 0.0 copy-done
  178.4 0.7 copy.11
Async XLA Ops:
  175.0 2.7 %copy-start.1 = (bf16[8,128,128]{2,1,0:T(8,128)(2,1)S(1)}, bf16[8,128,128]{2,1,0:T(8,128)(2,1)}, u32[]{:S(2)}) copy-start(bf16[8,128,128]{2,1,0:T(8,128)(2,1)} %get-tuple-element.7) | copy-start | bytes 786436
  175.0 3.4 %copy-start = (bf16[8,128,128]{2,1,0:T(8,128)(2,1)S(1)}, bf16[8,128,128]{2,1,0:T(8,128)(2,1)}, u32[]{:S(2)}) copy-start(bf16[8,128,128]{2,1,0:T(8,128)(2,1)} %get-tuple-element.8) | copy-start | bytes 786436
